TPU v7x, 128 devices: a whole 4x4x4 slice. The times are simulated.
128 devices in a mesh: gz: 32 (over x, z, y_lo), gx: 4 (over y_hi, core).
Axes of the slice: x: 4, y: 4 (y_hi: 2, y_lo: 2; y = y_hi * 2 + y_lo), z: 4, core: 2. Of those that a mesh axis runs over, the one named last changes fastest.
Arguments:
- velocity: float32 [256, 512, 512], P('gz', 'gx'), may hold values from -8 to 8
Outputs:
- detail_one: float32 [7, 128, 256, 256], P(None, 'gz', 'gx')
- detail_two: float32 [7, 64, 128, 128], P(None, 'gz', 'gx')
- detail_three: float32 [7, 32, 64, 64], P(None, 'gz', 'gx')
- coarse: float32 [32, 64, 64], P('gz', 'gx')
All inputs are finite; a program needn't handle non-finite values.
Results may differ from a plain program's by a relative error of at most 0.00002.
Values sent between devices are 32-bit elements; how exact they have to be, the bound alone decides.
A program may use at most 64 MiB of HBM per device.

v0:
```python
import jax
import jax.numpy as jnp
from jax import lax
from jax.sharding import PartitionSpec as P

LEVELS = 3


LOW_TAPS = (
    0.026748757411,
    -0.016864118443,
    -0.078223266529,
    0.266864118443,
    0.602949018236,
    0.266864118443,
    -0.078223266529,
    -0.016864118443,
    0.026748757411,
)
HIGH_TAPS = (
    0.091271763114,
    -0.057543526229,
    -0.591271763114,
    1.115087052457,
    -0.591271763114,
    -0.057543526229,
    0.091271763114,
)


def shifted(value, axis, steps):
    count = lax.axis_size(axis)
    pairs = [(source, (source + steps) % count) for source in range(count)]
    return lax.ppermute(value, axis, pairs)


def wrap_extend(field, along):
    count = field.shape[along]
    return jnp.concatenate(
        [
            lax.slice_in_dim(field, count - 4, count, axis=along),
            field,
            lax.slice_in_dim(field, 0, 3, axis=along),
        ],
        along,
    )


def split_bands(extended, along, length):
    widths = [(0, 0)] * extended.ndim
    widths[along] = (0, 1)
    padded = jnp.pad(extended, widths)
    half = length // 2
    shape = padded.shape[:along] + (half + 4, 2) + padded.shape[along + 1 :]
    phases = padded.reshape(shape)
    even_part = lax.index_in_dim(phases, 0, along + 1, keepdims=False)
    odd_part = lax.index_in_dim(phases, 1, along + 1, keepdims=False)
    low_band = jnp.zeros_like(lax.slice_in_dim(even_part, 0, half, axis=along))
    high_band = jnp.zeros_like(low_band)
    for offset in range(9):
        source = even_part if offset % 2 == 0 else odd_part
        start = offset // 2
        taken = lax.slice_in_dim(source, start, start + half, axis=along)
        low_band = low_band + LOW_TAPS[offset] * taken
        if offset >= 2:
            high_band = high_band + HIGH_TAPS[offset - 2] * taken
    return jnp.stack([low_band, high_band], 0)


def move_planes(piece, distance):
    if distance > 0:
        return shifted(piece, "gz", distance)
    return shifted(piece, "gz", distance)


def move_columns(piece, distance):
    if distance > 0:
        return shifted(piece, "gx", distance)
    return shifted(piece, "gx", distance)


def extend_rims(field, along, mover):
    count = field.shape[along]
    lower_parts = []
    needed = 4
    distance = 1
    while needed > 0:
        taken = min(count, needed)
        lower_parts.insert(
            0, mover(lax.slice_in_dim(field, count - taken, count, axis=along), distance)
        )
        needed = needed - taken
        distance = distance + 1
    upper_parts = []
    needed = 3
    distance = 1
    while needed > 0:
        taken = min(count, needed)
        upper_parts.append(mover(lax.slice_in_dim(field, 0, taken, axis=along), -distance))
        needed = needed - taken
        distance = distance + 1
    return jnp.concatenate(lower_parts + [field] + upper_parts, along)


def rim_bands(field):
    return split_bands(extend_rims(field, 0, move_planes), 0, field.shape[0])


def on_device(velocity):
    approx = velocity
    details = []
    for level_number in range(LEVELS):
        if level_number == 0:
            zbands = rim_bands(approx)
        elif level_number == LEVELS - 1:
            zbands = rim_bands(approx)
        else:
            zbands = rim_bands(approx)
        xbands = split_bands(extend_rims(zbands, 2, move_columns), 2, approx.shape[1])
        ybands = split_bands(wrap_extend(xbands, 4), 4, approx.shape[2])
        bands = ybands.reshape((8,) + ybands.shape[3:])
        details.append(bands[1:])
        approx = bands[0]
    return (details[0], details[1], details[2], approx)


def solution(mesh):
    placed = (P("gz", "gx", None),)
    return jax.shard_map(
        on_device,
        mesh=mesh,
        in_specs=placed,
        out_specs=(
            P(None, "gz", "gx", None),
            P(None, "gz", "gx", None),
            P(None, "gz", "gx", None),
            P("gz", "gx", None),
        ),
        check_vma=False,
    )
```

profile of v0, /device:TPU:1, one launch (start us, length us, event | category | flops | bytes accessed | tf_op | source)
XLA Modules:
  0.0 143.1 jit_solution(12949419969103555615)
XLA Ops:
  0.6 1.4 %slice.413 = f32[4,128,512]{2,1,0:T(8,128)S(1)} slice(f32[8,128,512]{2,1,0:T(8,128)} %param.1), slice={[4:8], [0:128], [0:512]} | slice | bytes 2097152 | tf_op jit(solution)/shard_map/slice | solution.py:90
  2.1 2.2 %collective-permute-start = (f32[4,128,512]{2,1,0:T(8,128)S(1)}, f32[4,128,512]{2,1,0:T(8,128)S(1)}, u32[]{:S(2)}, u32[]{:S(2)}) collective-permute-start(f32[4,128,512]{2,1,0:T(8,128)S(1)} %slice.413), channel_id=1, source_target_pairs={{0,4},{4,8},{8,12},{12,16},{16,20},{20,24},{24,28},{28,32},{32,36}... | collective-permute-start | bytes 3145736 | tf_op jit(solution)/shard_map/ppermute | solution.py:34
  4.3 6.1 %collective-permute-start.1 = (f32[3,128,512]{2,1,0:T(8,128)S(1)}, f32[3,128,512]{2,1,0:T(8,128)S(1)}, u32[]{:S(2)}, u32[]{:S(2)}) collective-permute-start(f32[3,128,512]{2,1,0:T(8,128)S(1)} %slice.414), channel_id=1, source_target_pairs={{0,124},{4,0},{8,4},{12,8},{16,12},{20,16},{24,20},{28,24},{32,28}... | collective-permute-start | bytes 2359304 | tf_op jit(solution)/shard_map/ppermute | solution.py:34
  10.4 34.8 %collective-permute-done.1 = f32[3,128,512]{2,1,0:T(8,128)S(1)} collective-permute-done((f32[3,128,512]{2,1,0:T(8,128)S(1)}, f32[3,128,512]{2,1,0:T(8,128)S(1)}, u32[]{:S(2)}, u32[]{:S(2)}) %collective-permute-start.1) | collective-permute-done | bytes 786464 | tf_op jit(solution)/shard_map/ppermute | solution.py:34
  45.2 0.7 select_maximum_fusion
  45.9 1.4 fusion.85
  47.3 10.0 %fusion.30 = (f32[1,4,128,512]{3,1,2,0:T(4,128)S(1)}, f32[1,4,128,512]{3,1,2,0:T(4,128)S(1)}) fusion(f32[4,1,128,512]{3,2,1,0:T(8,128)S(1)} %get-tuple-element.15, f32[4,1,128,512]{3,2,1,0:T(8,128)S(1)} %get-tuple-element.8, f32[4,1,128,512]{3,2,1,0:T(8,128)S(1)} %get-tuple-element.16, f32[4,1,128,512]{3,2,1,0:T(8,128)S(1)} %get-tuple-element.9, ...), kind=kLoop, calls=%fused_computation.50 | loop fusion | flops 7864320 | bytes 11534336 | tf_op jit(solution)/shard_map/add | solution.py:64
  57.4 4.4 %collective-permute-start.2 = (f32[2,4,4,512]{3,1,2,0:T(4,128)S(1)}, f32[2,4,4,512]{3,1,2,0:T(4,128)S(1)}, u32[]{:S(2)}, u32[]{:S(2)}) collective-permute-start(f32[2,4,4,512]{3,1,2,0:T(4,128)S(1)} %pad_maximum_fusion.7), channel_id=1, source_target_pairs={{0,1},{1,2},{2,3},{3,0},{4,5},{5,6},{6,7},{7,4},{8,9},{9,10},{10,1... | collective-permute-start | bytes 196616 | tf_op jit(solution)/shard_map/ppermute | solution.py:34
  61.8 0.3 collective-permute-start.3
  62.1 5.0 %collective-permute-done.3 = f32[2,4,3,512]{3,1,2,0:T(4,128)S(1)} collective-permute-done((f32[2,4,3,512]{3,1,2,0:T(4,128)S(1)}, f32[2,4,3,512]{3,1,2,0:T(4,128)S(1)}, u32[]{:S(2)}, u32[]{:S(2)}) %collective-permute-start.3) | collective-permute-done | bytes 49184 | tf_op jit(solution)/shard_map/ppermute | solution.py:34
  67.1 0.5 select_maximum_fusion.2
  67.6 0.4 slice_bitcast_fusion
  68.0 2.7 %fusion.31 = (f32[1,2,4,64,512]{4,2,3,1,0:T(4,128)S(1)}, f32[1,2,4,64,512]{4,2,3,1,0:T(4,128)S(1)}) fusion(f32[2,4,68,512]{3,1,2,0:T(4,128)S(1)} %get-tuple-element.21, f32[2,4,68,512]{3,1,2,0:T(4,128)S(1)} %get-tuple-element.22), kind=kLoop, calls=%fused_computation.51 | loop fusion | flops 7864320 | bytes 11534336 | tf_op jit(solution)/shard_map/stack | solution.py:67
  70.7 3.3 %fusion = f32[2,2,4,64,519]{4,2,3,1,0:T(4,128)S(1)} fusion(f32[1,2,4,64,512]{4,2,3,1,0:T(4,128)S(1)} %get-tuple-element.20, f32[1,2,4,64,512]{4,2,3,1,0:T(4,128)S(1)} %get-tuple-element.19), kind=kLoop, calls=%fused_computation.4 | loop fusion | flops 2657280 | bytes 4222976 | tf_op jit(solution)/shard_map/concatenate | solution.py:39
  74.0 3.3 %copy.243 = f32[2,2,4,64,519]{3,4,2,1,0:T(8,128)} copy(f32[2,2,4,64,519]{4,2,3,1,0:T(4,128)S(1)} %fusion) | data formatting | bytes 4251648
  77.3 2.5 %pad.38.clone = f32[2,2,4,64,520]{3,4,2,1,0:T(8,128)S(1)} pad(f32[2,2,4,64,519]{3,4,2,1,0:T(8,128)} %copy.243, f32[]{:T(128)} %constant.10.clone.1), padding=0_0x0_0x0_0x0_0x0_1 | pad | bytes 4255748 | tf_op jit(solution)/shard_map/jit(_pad)/pad | solution.py:52
  79.8 5.3 %fusion.84 = (f32[2,2,4,64,260,1]{3,5,4,2,1,0:T(1,128)}, f32[2,2,4,64,260,1]{3,5,4,2,1,0:T(1,128)}) fusion(f32[2,2,4,64,260,2]{3,5,4,2,1,0:T(2,128)S(1)} %bitcast.164), kind=kLoop, calls=%fused_computation.168 | loop fusion | bytes 4259840 | tf_op jit(solution)/shard_map/slice | solution.py:57
  85.1 4.7 %copy.191 = f32[2,2,4,64,260,1]{4,3,2,1,0,5:T(8,128)S(1)} copy(f32[2,2,4,64,260,1]{3,5,4,2,1,0:T(1,128)} %get-tuple-element.6) | data formatting | bytes 2129920 | tf_op jit(solution)/shard_map/slice | solution.py:57
  89.8 4.7 %copy.190 = f32[2,2,4,64,260,1]{4,3,2,1,0,5:T(8,128)S(1)} copy(f32[2,2,4,64,260,1]{3,5,4,2,1,0:T(1,128)} %get-tuple-element.7) | data formatting | bytes 2129920 | tf_op jit(solution)/shard_map/slice | solution.py:56
  94.5 2.0 %fusion.13 = (f32[1,2,2,4,64,256]{5,4,3,2,1,0:T(8,128)S(1)}, f32[1,2,2,4,64,256]{5,4,3,2,1,0:T(8,128)S(1)}) fusion(f32[2,2,4,64,260]{4,3,2,1,0:T(8,128)S(1)} %bitcast.163, f32[2,2,4,64,260]{4,3,2,1,0:T(8,128)S(1)} %bitcast.162), kind=kLoop, calls=%fused_computation.25 | loop fusion | flops 7864320 | bytes 11534336 | tf_op jit(solution)/shard_map/stack | solution.py:67
  96.4 0.2 pad_maximum_fusion.2
  96.7 0.5 collective-permute-start.4
  97.2 5.4 %collective-permute-start.5 = (f32[3,64,256]{2,1,0:T(8,128)S(1)}, f32[3,64,256]{2,1,0:T(8,128)S(1)}, u32[]{:S(2)}, u32[]{:S(2)}) collective-permute-start(f32[3,64,256]{2,1,0:T(8,128)S(1)} %slice_bitcast_fusion.3), channel_id=1, source_target_pairs={{0,124},{4,0},{8,4},{12,8},{16,12},{20,16},{24,20},{28,24},{32,28}... | collective-permute-start | bytes 589832 | tf_op jit(solution)/shard_map/ppermute | solution.py:34
  102.5 5.5 %collective-permute-done.5 = f32[3,64,256]{2,1,0:T(8,128)S(1)} collective-permute-done((f32[3,64,256]{2,1,0:T(8,128)S(1)}, f32[3,64,256]{2,1,0:T(8,128)S(1)}, u32[]{:S(2)}, u32[]{:S(2)}) %collective-permute-start.5) | collective-permute-done | bytes 196640 | tf_op jit(solution)/shard_map/ppermute | solution.py:34
  108.2 3.1 %collective-permute-start.6 = (f32[2,2,4,256]{3,2,1,0:T(4,128)S(1)}, f32[2,2,4,256]{3,2,1,0:T(4,128)S(1)}, u32[]{:S(2)}, u32[]{:S(2)}) collective-permute-start(f32[2,2,4,256]{3,2,1,0:T(4,128)S(1)} %pad_maximum_fusion.11), channel_id=1, source_target_pairs={{0,1},{1,2},{2,3},{3,0},{4,5},{5,6},{6,7},{7,4},{8,9},{9,10},{10,1... | collective-permute-start | bytes 49160 | tf_op jit(solution)/shard_map/ppermute | solution.py:34
  111.3 4.7 %collective-permute-done.7 = f32[2,2,3,256]{3,2,1,0:T(4,128)S(1)} collective-permute-done((f32[2,2,3,256]{3,2,1,0:T(4,128)S(1)}, f32[2,2,3,256]{3,2,1,0:T(4,128)S(1)}, u32[]{:S(2)}, u32[]{:S(2)}) %collective-permute-start.7) | collective-permute-done | bytes 12320 | tf_op jit(solution)/shard_map/ppermute | solution.py:34
  116.0 0.2 copy.244
  116.4 0.4 add_bitcast_fusion.5
  116.8 0.2 fusion.33
  117.0 1.4 fusion.32
  118.4 1.4 copy.245
  119.8 1.6 %fusion.86 = (f32[2,2,2,32,132,1]{3,5,4,2,1,0:T(1,128)S(1)}, f32[2,2,2,32,132,1]{3,5,4,2,1,0:T(1,128)}) fusion(f32[2,2,2,32,132,2]{3,5,4,2,1,0:T(2,128)S(1)} %bitcast.171), kind=kLoop, calls=%fused_computation.170 | loop fusion | bytes 540672 | tf_op jit(solution)/shard_map/slice | solution.py:57
  121.4 1.3 copy.205
  122.8 0.4 copy.206
  123.2 0.3 fusion.44
  123.5 1.4 collective-permute-start.8
  125.0 0.5 collective-permute-start.9
  125.5 5.2 %collective-permute-start.10 = (f32[2,32,128]{2,1,0:T(8,128)S(1)}, f32[2,32,128]{2,1,0:T(8,128)S(1)}, u32[]{:S(2)}, u32[]{:S(2)}) collective-permute-start(f32[2,32,128]{2,1,0:T(8,128)S(1)} %slice_bitcast_fusion.16), channel_id=1, source_target_pairs={{0,124},{4,0},{8,4},{12,8},{16,12},{20,16},{24,20},{28,24},{32,28}... | collective-permute-start | bytes 98312 | tf_op jit(solution)/shard_map/ppermute | solution.py:34
  130.8 1.2 collective-permute-done.9
  132.0 1.3 collective-permute-done.11
  133.3 2.1 %collective-permute-start.12 = (f32[2,1,4,128]{3,2,1,0:T(4,128)S(1)}, f32[2,1,4,128]{3,2,1,0:T(4,128)S(1)}, u32[]{:S(2)}, u32[]{:S(2)}) collective-permute-start(f32[2,1,4,128]{3,2,1,0:T(4,128)S(1)} %pad_maximum_fusion.13), channel_id=1, source_target_pairs={{0,1},{1,2},{2,3},{3,0},{4,5},{5,6},{6,7},{7,4},{8,9},{9,10},{10,1... | collective-permute-start | bytes 12296 | tf_op jit(solution)/shard_map/ppermute | solution.py:34
  135.4 1.4 slice.561
  136.8 0.7 slice.597
  137.5 2.5 %collective-permute-done.13 = f32[2,1,3,128]{3,2,1,0:T(4,128)S(1)} collective-permute-done((f32[2,1,3,128]{3,2,1,0:T(4,128)S(1)}, f32[2,1,3,128]{3,2,1,0:T(4,128)S(1)}, u32[]{:S(2)}, u32[]{:S(2)}) %collective-permute-start.13) | collective-permute-done | bytes 3104 | tf_op jit(solution)/shard_map/ppermute | solution.py:34
  140.5 0.1 slice_bitcast_fusion.6
  140.8 0.9 multiply_add_fusion.1
  141.9 0.6 slice.633
  142.5 0.6 slice_bitcast_fusion.19
  (53 shorter events, 1.6 us)
Async XLA Ops:
  0.6 3.6 %copy-start = (f32[8,128,512]{2,1,0:T(8,128)S(1)}, f32[8,128,512]{2,1,0:T(8,128)}, u32[]{:S(2)}) copy-start(f32[8,128,512]{2,1,0:T(8,128)} %param.1) | copy-start | bytes 6291460
  2.1 43.1 %collective-permute-start = (f32[4,128,512]{2,1,0:T(8,128)S(1)}, f32[4,128,512]{2,1,0:T(8,128)S(1)}, u32[]{:S(2)}, u32[]{:S(2)}) collective-permute-start(f32[4,128,512]{2,1,0:T(8,128)S(1)} %slice.413), channel_id=1, source_target_pairs={{0,4},{4,8},{8,12},{12,16},{16,20},{20,24},{24,28},{28,32},{32,36}... | collective-permute-start | bytes 3145736 | tf_op jit(solution)/shard_map/ppermute | solution.py:34
  4.3 40.9 %collective-permute-start.1 = (f32[3,128,512]{2,1,0:T(8,128)S(1)}, f32[3,128,512]{2,1,0:T(8,128)S(1)}, u32[]{:S(2)}, u32[]{:S(2)}) collective-permute-start(f32[3,128,512]{2,1,0:T(8,128)S(1)} %slice.414), channel_id=1, source_target_pairs={{0,124},{4,0},{8,4},{12,8},{16,12},{20,16},{24,20},{28,24},{32,28}... | collective-permute-start | bytes 2359304 | tf_op jit(solution)/shard_map/ppermute | solution.py:34
  57.4 9.7 %collective-permute-start.2 = (f32[2,4,4,512]{3,1,2,0:T(4,128)S(1)}, f32[2,4,4,512]{3,1,2,0:T(4,128)S(1)}, u32[]{:S(2)}, u32[]{:S(2)}) collective-permute-start(f32[2,4,4,512]{3,1,2,0:T(4,128)S(1)} %pad_maximum_fusion.7), channel_id=1, source_target_pairs={{0,1},{1,2},{2,3},{3,0},{4,5},{5,6},{6,7},{7,4},{8,9},{9,10},{10,1... | collective-permute-start | bytes 196616 | tf_op jit(solution)/shard_map/ppermute | solution.py:34
  61.8 5.3 %collective-permute-start.3 = (f32[2,4,3,512]{3,1,2,0:T(4,128)S(1)}, f32[2,4,3,512]{3,1,2,0:T(4,128)S(1)}, u32[]{:S(2)}, u32[]{:S(2)}) collective-permute-start(f32[2,4,3,512]{3,1,2,0:T(4,128)S(1)} %pad_maximum_fusion.9), channel_id=1, source_target_pairs={{0,3},{1,0},{2,1},{3,2},{4,7},{5,4},{6,5},{7,6},{8,11},{9,8},{10,9... | collective-permute-start | bytes 147464 | tf_op jit(solution)/shard_map/ppermute | solution.py:34
  96.7 11.3 %collective-permute-start.4 = (f32[4,64,256]{2,1,0:T(8,128)S(1)}, f32[4,64,256]{2,1,0:T(8,128)S(1)}, u32[]{:S(2)}, u32[]{:S(2)}) collective-permute-start(f32[4,64,256]{2,1,0:T(8,128)S(1)} %slice_bitcast_fusion.2), channel_id=1, source_target_pairs={{0,4},{4,8},{8,12},{12,16},{16,20},{20,24},{24,28},{28,32},{32,36}... | collective-permute-start | bytes 786440 | tf_op jit(solution)/shard_map/ppermute | solution.py:34
  97.2 10.8 %collective-permute-start.5 = (f32[3,64,256]{2,1,0:T(8,128)S(1)}, f32[3,64,256]{2,1,0:T(8,128)S(1)}, u32[]{:S(2)}, u32[]{:S(2)}) collective-permute-start(f32[3,64,256]{2,1,0:T(8,128)S(1)} %slice_bitcast_fusion.3), channel_id=1, source_target_pairs={{0,124},{4,0},{8,4},{12,8},{16,12},{20,16},{24,20},{28,24},{32,28}... | collective-permute-start | bytes 589832 | tf_op jit(solution)/shard_map/ppermute | solution.py:34
  108.2 7.7 %collective-permute-start.6 = (f32[2,2,4,256]{3,2,1,0:T(4,128)S(1)}, f32[2,2,4,256]{3,2,1,0:T(4,128)S(1)}, u32[]{:S(2)}, u32[]{:S(2)}) collective-permute-start(f32[2,2,4,256]{3,2,1,0:T(4,128)S(1)} %pad_maximum_fusion.11), channel_id=1, source_target_pairs={{0,1},{1,2},{2,3},{3,0},{4,5},{5,6},{6,7},{7,4},{8,9},{9,10},{10,1... | collective-permute-start | bytes 49160 | tf_op jit(solution)/shard_map/ppermute | solution.py:34
  111.3 4.7 %collective-permute-start.7 = (f32[2,2,3,256]{3,2,1,0:T(4,128)S(1)}, f32[2,2,3,256]{3,2,1,0:T(4,128)S(1)}, u32[]{:S(2)}, u32[]{:S(2)}) collective-permute-start(f32[2,2,3,256]{3,2,1,0:T(4,128)S(1)} %pad_maximum_fusion.10), channel_id=1, source_target_pairs={{0,3},{1,0},{2,1},{3,2},{4,7},{5,4},{6,5},{7,6},{8,11},{9,8},{10,9... | collective-permute-start | bytes 36872 | tf_op jit(solution)/shard_map/ppermute | solution.py:34
  123.5 7.2 %collective-permute-start.8 = (f32[2,32,128]{2,1,0:T(8,128)S(1)}, f32[2,32,128]{2,1,0:T(8,128)S(1)}, u32[]{:S(2)}, u32[]{:S(2)}) collective-permute-start(f32[2,32,128]{2,1,0:T(8,128)S(1)} %slice_bitcast_fusion.16), channel_id=1, source_target_pairs={{0,8},{4,12},{8,16},{12,20},{16,24},{20,28},{24,32},{28,36},{32,40... | collective-permute-start | bytes 98312 | tf_op jit(solution)/shard_map/ppermute | solution.py:34
  125.0 7.0 %collective-permute-start.9 = (f32[2,32,128]{2,1,0:T(8,128)S(1)}, f32[2,32,128]{2,1,0:T(8,128)S(1)}, u32[]{:S(2)}, u32[]{:S(2)}) collective-permute-start(f32[2,32,128]{2,1,0:T(8,128)S(1)} %slice_bitcast_fusion.16), channel_id=1, source_target_pairs={{0,4},{4,8},{8,12},{12,16},{16,20},{20,24},{24,28},{28,32},{32,36}... | collective-permute-start | bytes 98312 | tf_op jit(solution)/shard_map/ppermute | solution.py:34
  125.5 6.5 %collective-permute-start.10 = (f32[2,32,128]{2,1,0:T(8,128)S(1)}, f32[2,32,128]{2,1,0:T(8,128)S(1)}, u32[]{:S(2)}, u32[]{:S(2)}) collective-permute-start(f32[2,32,128]{2,1,0:T(8,128)S(1)} %slice_bitcast_fusion.16), channel_id=1, source_target_pairs={{0,124},{4,0},{8,4},{12,8},{16,12},{20,16},{24,20},{28,24},{32,28}... | collective-permute-start | bytes 98312 | tf_op jit(solution)/shard_map/ppermute | solution.py:34
  130.6 2.6 %collective-permute-start.11 = (f32[1,32,128]{2,1,0:T(8,128)S(1)}, f32[1,32,128]{2,1,0:T(8,128)S(1)}, u32[]{:S(2)}, u32[]{:S(2)}) collective-permute-start(f32[1,32,128]{2,1,0:T(8,128)S(1)} %slice_bitcast_fusion.18), channel_id=1, source_target_pairs={{0,120},{4,124},{8,0},{12,4},{16,8},{20,12},{24,16},{28,20},{32,24... | collective-permute-start | bytes 49160 | tf_op jit(solution)/shard_map/ppermute | solution.py:34
  133.3 6.7 %collective-permute-start.12 = (f32[2,1,4,128]{3,2,1,0:T(4,128)S(1)}, f32[2,1,4,128]{3,2,1,0:T(4,128)S(1)}, u32[]{:S(2)}, u32[]{:S(2)}) collective-permute-start(f32[2,1,4,128]{3,2,1,0:T(4,128)S(1)} %pad_maximum_fusion.13), channel_id=1, source_target_pairs={{0,1},{1,2},{2,3},{3,0},{4,5},{5,6},{6,7},{7,4},{8,9},{9,10},{10,1... | collective-permute-start | bytes 12296 | tf_op jit(solution)/shard_map/ppermute | solution.py:34
  135.4 4.5 %collective-permute-start.13 = (f32[2,1,3,128]{3,2,1,0:T(4,128)S(1)}, f32[2,1,3,128]{3,2,1,0:T(4,128)S(1)}, u32[]{:S(2)}, u32[]{:S(2)}) collective-permute-start(f32[2,1,3,128]{3,2,1,0:T(4,128)S(1)} %pad_maximum_fusion.12), channel_id=1, source_target_pairs={{0,3},{1,0},{2,1},{3,2},{4,7},{5,4},{6,5},{7,6},{8,11},{9,8},{10,9... | collective-permute-start | bytes 9224 | tf_op jit(solution)/shard_map/ppermute | solution.py:34
where the time goes:
time: 143 us
  waiting for transfers between devices  54.8 us (38%)
  local copies, waits for them, and re-layouts  32.9 us (23%)
  starting transfers between devices  31.2 us (22%)
  other arithmetic  23.1 us (16%)
    ppermute x14, waiting for transfers between devices, shifted(): return lax.ppermute(value, axis, pairs)  54.8 us
    ppermute x14, starting transfers between devices, shifted(): return lax.ppermute(value, axis, pairs)  31.2 us
    slice x4, local copies, waits for them, and re-layouts, split_bands(): odd_part = lax.index_in_dim(phases, 1, along + 1, keepdims=False)  12 us
    add x4, other arithmetic, split_bands(): low_band = low_band + LOW_TAPS[offset] * taken  11 us
    slice x2, local copies, waits for them, and re-layouts, split_bands(): even_part = lax.index_in_dim(phases, 0, along + 1, keepdims=False)  6 us
    another operation x13, other arithmetic, split_bands(): return jnp.stack([low_band, high_band], 0)  5.89 us
    unnamed x11, local copies, waits for them, and re-layouts  4.96 us
    concatenate x3, other arithmetic, wrap_extend(): jnp.concatenate([lax.slice_in_dim(field, count - 4, count, axis=along), f...  4.79 us
  transfers between devices with their start and end apart: 14, of which 7 were waited for; matrix products, arithmetic and copies ran while one was open for 2% of the time, Pallas kernels for 0%

commit v1 on v0

v1 whole, which is shorter than its diff:
```python
import functools

import jax
import jax.numpy as jnp
import numpy as np
from jax import lax
from jax.experimental import pallas as pl
from jax.experimental.pallas import tpu as pltpu
from jax.sharding import PartitionSpec as P

LOW_TAPS = (
    0.026748757411,
    -0.016864118443,
    -0.078223266529,
    0.266864118443,
    0.602949018236,
    0.266864118443,
    -0.078223266529,
    -0.016864118443,
    0.026748757411,
)
HIGH_TAPS = (
    0.091271763114,
    -0.057543526229,
    -0.591271763114,
    1.115087052457,
    -0.591271763114,
    -0.057543526229,
    0.091271763114,
)

AL = -1.586134342059924
BE = -0.052980118572961
GA = 0.882911075530934
DE = 0.443506852043971
KL = 1.0 / 1.230174104914001
KH = 1.230174104914001
SCALE = (KL, KH)

MESH = pl.DeviceIdType.MESH
HIGHEST = lax.Precision.HIGHEST


def band_matrix(n):
    half = n // 2
    w = np.zeros((n, n), np.float64)
    for j in range(half):
        for k in range(9):
            w[(2 * j + k - 4) % n, j] += LOW_TAPS[k]
        for k in range(7):
            w[(2 * j + 1 + k - 3) % n, half + j] += HIGH_TAPS[k]
    return w.astype(np.float32)


def edge_terms(get, n):
    a = get(n - 1) + AL * get(n - 2)
    b = get(n - 2) + BE * (get(n - 3) + AL * (get(n - 4) + get(n - 2)) + a)
    e = get(0)
    c = e + BE * (get(1) + AL * (e + get(2)))
    return a, b, e, c


def lift_planes(f, a, b, e_up, c):
    even, odd = f[0::2], f[1::2]
    n = len(even)
    even_next = even[1:] + [e_up]
    d1 = [odd[j] + AL * (even[j] + even_next[j]) for j in range(n)]
    d1m = a + AL * even[0]
    d1_prev = [d1m] + d1[:-1]
    s1 = [even[j] + BE * (d1_prev[j] + d1[j]) for j in range(n)]
    s1m = b + (AL * BE) * even[0]
    s1n = c + BE * d1[-1]
    s1_next = s1[1:] + [s1n]
    d2 = [d1[j] + GA * (s1[j] + s1_next[j]) for j in range(n)]
    d2m = d1m + GA * (s1m + s1[0])
    d2_prev = [d2m] + d2[:-1]
    s2 = [s1[j] + DE * (d2_prev[j] + d2[j]) for j in range(n)]
    return s2, d2


def from_above(x, row):
    n = x.shape[0]
    at = lax.broadcasted_iota(jnp.int32, x.shape, 0)
    return jnp.where(at == n - 1, row, pltpu.roll(x, n - 1, 0))


def from_below(x, row):
    at = lax.broadcasted_iota(jnp.int32, x.shape, 0)
    return jnp.where(at == 0, row, pltpu.roll(x, 1, 0))


def lift_rows(even, odd, a, b, e_up, c):
    n = even.shape[0]
    d1 = odd + AL * (even + from_above(even, e_up))
    d1m = a + AL * even[0:1]
    s1 = even + BE * (from_below(d1, d1m) + d1)
    s1m = b + (AL * BE) * even[0:1]
    s1n = c + BE * d1[n - 1 : n]
    d2 = d1 + GA * (s1 + from_above(s1, s1n))
    d2m = d1m + GA * (s1m + s1[0:1])
    s2 = s1 + DE * (from_below(d2, d2m) + d2)
    return s2, d2


def dot(x, w):
    return jnp.dot(x, w, precision=HIGHEST, preferred_element_type=jnp.float32)


def kernel(
    nz, nx,
    v_hbm, w1_hbm, w2_hbm, w3_hbm,
    one_hbm, two_hbm, three_hbm, coarse_hbm,
    f1, w1, w2, w3, y1, xs1, xr1, own1, zs1, zr1,
    f2, y2, xs2, xr2, own2, zs2, zr2,
    f3, y3, xs3, xr3, own3, zs3, zr3, zr3b,
    one, two, three, coarse,
    in_sem, out_sem, xsend, xrecv, zsend, zrecv,
):
    iz, ix = lax.axis_index("gz"), lax.axis_index("gx")
    right, left = lax.rem(ix + 1, nx), lax.rem(ix + nx - 1, nx)
    up, down = lax.rem(iz + 1, nz), lax.rem(iz + nz - 1, nz)
    up2, down2 = lax.rem(iz + 2, nz), lax.rem(iz + nz - 2, nz)

    barrier = pltpu.get_barrier_semaphore()
    for k in (right, left):
        pl.semaphore_signal(barrier, inc=1, device_id={"gx": k}, device_id_type=MESH)
    for k in (up, down, up2, down2):
        pl.semaphore_signal(barrier, inc=1, device_id={"gz": k}, device_id_type=MESH)

    loads = [
        pltpu.make_async_copy(src, dst, in_sem.at[i])
        for i, (src, dst) in enumerate(
            [(v_hbm, f1), (w1_hbm, w1), (w2_hbm, w2), (w3_hbm, w3)]
        )
    ]
    for load in loads:
        load.start()

    sent = []

    def send(src, dst, send_sem, recv_sem, device):
        copy = pltpu.make_async_remote_copy(
            src_ref=src, dst_ref=dst, send_sem=send_sem, recv_sem=recv_sem,
            device_id=device, device_id_type=MESH,
        )
        copy.start()
        sent.append(copy)
        return copy

    def send_x(level, xs, xr):
        return [
            send(xs.at[0:2], xr.at[0:2], xsend.at[level, 0], xrecv.at[level, 0], {"gx": right}),
            send(xs.at[2:4], xr.at[2:4], xsend.at[level, 1], xrecv.at[level, 1], {"gx": left}),
        ]

    def send_z(slot, zs, zr, groups):
        return [
            send(zs.at[0, groups], zr.at[0, groups], zsend.at[slot, 0], zrecv.at[slot, 0], {"gz": up}),
            send(zs.at[1, groups], zr.at[1, groups], zsend.at[slot, 1], zrecv.at[slot, 1], {"gz": down}),
        ]

    stores = []

    def store(src, dst):
        copy = pltpu.make_async_copy(src, dst, out_sem.at[len(stores)])
        copy.start()
        stores.append(copy)

    def arrive(copies):
        for copy in copies:
            copy.wait_recv()

    def x_split(y, xr, own, columns):
        planes, half = y.shape[1], y.shape[2] // 2
        wide = max(1, y.shape[0] // 2)

        def plane(p):
            for column in columns:
                yb, at = column // wide, 128 * (column % wide)
                even = y[column, p, pl.ds(0, half, stride=2), :]
                odd = y[column, p, pl.ds(1, half, stride=2), :]
                terms = [xr[k, column, pl.ds(p, 1), :] for k in range(4)]
                low, high = lift_rows(even, odd, *terms)
                own[2 * yb, p, :, pl.ds(at, 128)] = low
                own[2 * yb + 1, p, :, pl.ds(at, 128)] = high

        if planes == 8:
            lax.fori_loop(0, planes, lambda p, _: (plane(p), 0)[1], 0)
        else:
            for p in range(planes):
                plane(p)

    def z_terms(own, zs, groups, step):
        planes, rows = own.shape[1], own.shape[2]
        for g in groups:
            def chunk(i, _):
                at = pl.ds(pl.multiple_of(i * step, step), step)
                terms = edge_terms(lambda k: own[g, k, at, :], planes)
                for k in range(4):
                    zs[k // 2, g, k % 2, at, :] = terms[k]
                return 0

            lax.fori_loop(0, rows // step, chunk, 0)

    def z_split(own, zr, g, step, low_to, high_to):
        planes, rows = own.shape[1], own.shape[2]

        def chunk(i, _):
            at = pl.ds(pl.multiple_of(i * step, step), step)
            f = [own[g, k, at, :] for k in range(planes)]
            terms = [zr[k // 2, g, k % 2, at, :] for k in range(4)]
            low, high = lift_planes(f, *terms)
            for j in range(planes // 2):
                low_to[j, at, :] = low[j] * (KL * SCALE[g % 2])
                high_to[j, at, :] = high[j] * (KH * SCALE[g % 2])
            return 0

        lax.fori_loop(0, rows // step, chunk, 0)

    def bands(out, g):
        return out.at[2 * g - 1], out.at[2 * g]

    loads[0].wait()
    loads[1].wait()
    edges = edge_terms(lambda k: f1[:, k, :], f1.shape[1])
    out = dot(jnp.concatenate(edges, 0), w1[...])
    for k in range(4):
        for c in range(4):
            xs1[k, c] = out[8 * k : 8 * k + 8, 128 * c : 128 * c + 128]
    pl.semaphore_wait(barrier, 6)
    x1 = send_x(0, xs1, xr1)
    planes = f1.shape[0]
    for yb in range(2):
        lanes = pl.ds(256 * yb, 256)

        def rows(i, _):
            at = pl.ds(2 * i, 2)
            out = dot(f1[at].reshape(256, 512), w1[:, lanes])
            for c in range(2):
                y1[2 * yb + c, at] = out[:, 128 * c : 128 * c + 128].reshape(2, 128, 128)
            return 0

        lax.fori_loop(0, planes // 2, rows, 0)
        if yb == 0:
            arrive(x1)
        x_split(y1, xr1, own1, (2 * yb, 2 * yb + 1))
        z_terms(own1, zs1, (2 * yb, 2 * yb + 1), 16)
        if yb == 0:
            z1 = [send_z(0, zs1, zr1, 0), send_z(1, zs1, zr1, 1)]
        else:
            z1 += [send_z(2, zs1, zr1, 2), send_z(3, zs1, zr1, 3)]

    arrive(z1[0])
    z_split(own1, zr1, 0, 8, f2, one.at[0])
    store(one.at[0:1], one_hbm.at[0:1])

    loads[2].wait()
    out = dot(f2[...].reshape(256, 256), w2[...])
    for c in range(2):
        y2[c] = out[:, 128 * c : 128 * c + 128].reshape(4, 64, 128)
        for k, term in enumerate(edge_terms(lambda k: y2[c, :, k, :], 64)):
            xs2[k, c] = term
    x2 = send_x(1, xs2, xr2)
    arrive(x2)
    x_split(y2, xr2, own2, (0, 1))
    z_terms(own2, zs2, range(4), 32)
    z2 = [send_z(4, zs2, zr2, 0), send_z(5, zs2, zr2, pl.ds(1, 3))]
    arrive(z2[0])
    z_split(own2, zr2, 0, 32, f3, two.at[0])
    store(two.at[0:1], two_hbm.at[0:1])

    loads[3].wait()
    y3[0] = dot(f3[...].reshape(64, 128), w3[...]).reshape(2, 32, 128)
    for k, term in enumerate(edge_terms(lambda k: y3[0, :, k, :], 32)):
        xs3[k, 0] = term
    x3 = send_x(2, xs3, xr3)
    arrive(x3)
    x_split(y3, xr3, own3, (0,))
    for xb in range(2):
        even, odd = own3[xb, 0], own3[xb, 1]
        a = odd + AL * even
        zs3[0, xb] = a
        zs3[1, xb] = even + BE * (AL * even + a)
        zs3[2, xb] = even
        zs3[3, xb] = even + BE * (odd + AL * even)
    z3 = [
        send(zs3.at[0:2], zr3.at[0:2], zsend.at[6, 0], zrecv.at[6, 0], {"gz": up}),
        send(zs3.at[2:4], zr3.at[2:4], zsend.at[6, 1], zrecv.at[6, 1], {"gz": down}),
        send(zs3.at[0:1], zr3b.at[0:1], zsend.at[7, 0], zrecv.at[7, 0], {"gz": up2}),
        send(zs3.at[2:3], zr3b.at[1:2], zsend.at[7, 1], zrecv.at[7, 1], {"gz": down2}),
    ]
    for g in (1, 2):
        arrive(z1[g])
        z_split(own1, zr1, g, 8, *bands(one, g))
        store(one.at[2 * g - 1 : 2 * g + 1], one_hbm.at[2 * g - 1 : 2 * g + 1])
    arrive(z3)
    for xb in range(2):
        a, b, e, c = (zr3[k, xb] for k in range(4))
        b = b + BE * zr3b[0, xb]
        c = c + (AL * BE) * zr3b[1, xb]
        low, high = lift_planes([own3[xb, 0], own3[xb, 1]], a, b, e, c)
        low, high = low[0] * (KL * SCALE[xb]), high[0] * (KH * SCALE[xb])
        for yb in range(2):
            lanes = slice(64 * yb, 64 * yb + 64)
            band = 2 * xb + 4 * yb
            if band == 0:
                coarse[0] = low[:, lanes]
            else:
                three[band - 1, 0] = low[:, lanes]
            three[band, 0] = high[:, lanes]
    store(coarse, coarse_hbm)
    store(three, three_hbm)
    arrive(z2[1])
    for g in (1, 2, 3):
        z_split(own2, zr2, g, 32, *bands(two, g))
    store(two.at[1:7], two_hbm.at[1:7])
    arrive(z1[3])
    z_split(own1, zr1, 3, 8, *bands(one, 3))
    store(one.at[5:7], one_hbm.at[5:7])
    for copy in sent:
        copy.wait_send()
    for copy in stores:
        copy.wait()


def on_device(nz, nx, velocity):
    f32 = jnp.float32
    shapes = [(7, 4, 64, 256), (7, 2, 32, 128), (7, 1, 16, 64), (1, 16, 64)]
    scratch = [
        (8, 128, 512), (512, 512), (256, 256), (128, 128),
        (4, 8, 128, 128), (4, 4, 8, 128), (4, 4, 8, 128), (4, 8, 64, 256), (2, 4, 2, 64, 256), (2, 4, 2, 64, 256),
        (4, 64, 256), (2, 4, 64, 128), (4, 2, 4, 128), (4, 2, 4, 128), (4, 4, 32, 128), (2, 4, 2, 32, 128), (2, 4, 2, 32, 128),
        (2, 32, 128), (1, 2, 32, 128), (4, 1, 2, 128), (4, 1, 2, 128), (2, 2, 16, 128), (4, 2, 16, 128), (4, 2, 16, 128), (2, 2, 16, 128),
    ] + shapes
    dma = pltpu.SemaphoreType.DMA
    hbm = pl.BlockSpec(memory_space=pl.ANY)
    return pl.pallas_call(
        functools.partial(kernel, nz, nx),
        out_shape=tuple(jax.ShapeDtypeStruct(s, f32) for s in shapes),
        in_specs=[hbm] * 4,
        out_specs=(hbm,) * 4,
        scratch_shapes=[pltpu.VMEM(s, f32) for s in scratch]
        + [dma((4,)), dma((8,)), dma((3, 2)), dma((3, 2)), dma((8, 2)), dma((8, 2))],
        compiler_params=pltpu.CompilerParams(collective_id=0, has_side_effects=True),
        name="wavelet",
    )(velocity, *(jnp.asarray(band_matrix(n)) for n in (512, 256, 128)))


def solution(mesh):
    return jax.shard_map(
        functools.partial(on_device, mesh.shape["gz"], mesh.shape["gx"]),
        mesh=mesh,
        in_specs=(P("gz", "gx", None),),
        out_specs=(
            P(None, "gz", "gx", None),
            P(None, "gz", "gx", None),
            P(None, "gz", "gx", None),
            P("gz", "gx", None),
        ),
        check_vma=False,
    )
```

time: 143 us -> 58.5 us (0.41)
  waiting for transfers between devices: 54.8 us -> 0 us
  Pallas kernels: 0 us -> 52.8 us
  starting transfers between devices: 31.2 us -> 0 us
  local copies, waits for them, and re-layouts: 32.9 us -> 4.89 us
  other arithmetic: 23.1 us -> 0 us
    ppermute x14 -> x0, waiting for transfers between devices: 54.8 us -> none  [shifted(): return lax.ppermute(value, axis, pairs)]
    pallas_call x0 -> x1, Pallas kernels: none -> 52.8 us  [on_device(): pl.pallas_call(functools.partial(kernel, nz, nx), out_shape=tuple((jax.Sh...]
    ppermute x14 -> x0, starting transfers between devices: 31.2 us -> none  [shifted(): return lax.ppermute(value, axis, pairs)]
    slice x15 -> x0, local copies, waits for them, and re-layouts: 23.7 us -> none  [the longest x4 12 us: split_bands(): odd_part = lax.index_in_dim(phases, 1, along + 1, keepdims=False)]
    add x6 -> x0, other arithmetic: 11.1 us -> none  [the longest x4 11 us: split_bands(): low_band = low_band + LOW_TAPS[offset] * taken]
    concatenate x8 -> x0, other arithmetic: 6.1 us -> none  [the longest x3 4.79 us: wrap_extend(): jnp.concatenate([lax.slice_in_dim(field, count - 4, count, axis=along), f...]
    another operation x13 -> x0, other arithmetic: 5.89 us -> none  [split_bands(): return jnp.stack([low_band, high_band], 0)]
    pad x5 -> x0, local copies, waits for them, and re-layouts: 2.69 us -> none  [split_bands(): padded = jnp.pad(extended, widths)]
  transfers between devices with their start and end apart: 14 -> 0, of which waited for: 7 -> 0; matrix products, arithmetic and copies ran while one was open for 2% -> 0% of each run, Pallas kernels for 0% -> 0%
where the time goes in v1:
time: 58.5 us; the launch traced here: 58.4 us
  Pallas kernels  52.8 us (90%)
  local copies, waits for them, and re-layouts  4.89 us (8%)
  between operations  0.66 us (1%)
    pallas_call x1, Pallas kernels, on_device(): pl.pallas_call(functools.partial(kernel, nz, nx), out_shape=tuple((jax.Sh...  52.8 us
    unnamed x10, local copies, waits for them, and re-layouts  4.89 us

profile of v1, /device:TPU:1, one launch (start us, length us, event | category | flops | bytes accessed | tf_op | source)
XLA Modules:
  0.0 58.4 jit_solution(731089649520953364)
XLA Ops:
  0.6 52.8 %wavelet.1 = (f32[7,4,64,256]{3,2,1,0:T(8,128)}, f32[7,2,32,128]{3,2,1,0:T(8,128)}, f32[7,1,16,64]{3,2,1,0:T(8,128)}, f32[1,16,64]{2,1,0:T(8,128)}) custom-call(f32[8,128,512]{2,1,0:T(8,128)} %v_hbm.1, f32[512,512]{1,0:T(8,128)} %constant.6.clone.w1_hbm, f32[256,256]{1,0:T(8,128)} %constant.7.clone.w2_hbm, f32[128,128]{1,0:T(8,128)} %constant.8.clone.w3_hbm), custom_call_target="tpu_custom_call" | custom-call | tf_op jit(solution)/shard_map/wavelet/pallas_call | solution.py:337
  53.4 0.0 copy-start
  53.5 0.0 copy-start.1
  53.5 0.0 copy-start.2
  53.5 3.0 %copy.12 = f32[7,4,64,256]{3,2,1,0:T(8,128)} copy(f32[7,4,64,256]{3,2,1,0:T(8,128)} %get-tuple-element.8) | data formatting | bytes 3670016
  56.5 0.0 copy-done
  56.5 0.7 %copy.13 = f32[7,2,32,128]{3,2,1,0:T(8,128)} copy(f32[7,2,32,128]{3,2,1,0:T(8,128)S(1)} %copy-done) | data formatting | bytes 458752
  57.1 0.0 copy-done.1
  57.1 0.6 %copy.14 = f32[7,1,16,64]{3,2,1,0:T(8,128)} copy(f32[7,1,16,64]{3,2,1,0:T(8,128)S(1)} %copy-done.1) | data formatting | bytes 57344
  57.8 0.0 copy-done.2
  57.8 0.6 %copy.15 = f32[1,16,64]{2,1,0:T(8,128)} copy(f32[1,16,64]{2,1,0:T(8,128)S(1)} %copy-done.2) | data formatting | bytes 8192
Async XLA Ops:
  53.4 3.0 %copy-start = (f32[7,2,32,128]{3,2,1,0:T(8,128)S(1)}, f32[7,2,32,128]{3,2,1,0:T(8,128)}, u32[]{:S(2)}) copy-start(f32[7,2,32,128]{3,2,1,0:T(8,128)} %get-tuple-element.9) | copy-start | bytes 688132
  53.5 3.7 %copy-start.1 = (f32[7,1,16,64]{3,2,1,0:T(8,128)S(1)}, f32[7,1,16,64]{3,2,1,0:T(8,128)}, u32[]{:S(2)}) copy-start(f32[7,1,16,64]{3,2,1,0:T(8,128)} %get-tuple-element.10) | copy-start | bytes 86020
  53.5 4.3 %copy-start.2 = (f32[1,16,64]{2,1,0:T(8,128)S(1)}, f32[1,16,64]{2,1,0:T(8,128)}, u32[]{:S(2)}) copy-start(f32[1,16,64]{2,1,0:T(8,128)} %get-tuple-element.11) | copy-start | bytes 12292

commit v2 on v1

--- a/solution.py
+++ b/solution.py
@@ -109,12 +109,11 @@
 def kernel(
     nz, nx,
     v_hbm, w1_hbm, w2_hbm, w3_hbm,
-    one_hbm, two_hbm, three_hbm, coarse_hbm,
+    one, two, three, coarse,
     f1, w1, w2, w3, y1, xs1, xr1, own1, zs1, zr1,
     f2, y2, xs2, xr2, own2, zs2, zr2,
     f3, y3, xs3, xr3, own3, zs3, zr3, zr3b,
-    one, two, three, coarse,
-    in_sem, out_sem, xsend, xrecv, zsend, zrecv,
+    in_sem, xsend, xrecv, zsend, zrecv, usend, urecv,
 ):
     iz, ix = lax.axis_index("gz"), lax.axis_index("gx")
     right, left = lax.rem(ix + 1, nx), lax.rem(ix + nx - 1, nx)
@@ -159,12 +158,19 @@
             send(zs.at[1, groups], zr.at[1, groups], zsend.at[slot, 1], zrecv.at[slot, 1], {"gz": down}),
         ]
 
-    stores = []
-
-    def store(src, dst):
-        copy = pltpu.make_async_copy(src, dst, out_sem.at[len(stores)])
-        copy.start()
-        stores.append(copy)
+    units = [(g, k, r) for g in (1, 2, 3) for k in range(2) for r in range(2)]
+    pending = list(units)
+    on_way = {1: [], 2: [], 3: []}
+
+    def send_units(count):
+        for _ in range(min(count, len(pending))):
+            g, k, r = pending.pop(0)
+            at = pl.ds(32 * r, 32)
+            for d, device in ((0, {"gz": up}), (1, {"gz": down})):
+                i = units.index((g, k, r))
+                on_way[g].append(
+                    send(zs1.at[d, g, k, at], zr1.at[d, g, k, at], usend.at[i, d], urecv.at[i, d], device)
+                )
 
     def arrive(copies):
         for copy in copies:
@@ -246,13 +252,11 @@
         x_split(y1, xr1, own1, (2 * yb, 2 * yb + 1))
         z_terms(own1, zs1, (2 * yb, 2 * yb + 1), 16)
         if yb == 0:
-            z1 = [send_z(0, zs1, zr1, 0), send_z(1, zs1, zr1, 1)]
-        else:
-            z1 += [send_z(2, zs1, zr1, 2), send_z(3, zs1, zr1, 3)]
-
-    arrive(z1[0])
+            z1 = send_z(0, zs1, zr1, 0)
+            send_units(3)
+
+    arrive(z1)
     z_split(own1, zr1, 0, 8, f2, one.at[0])
-    store(one.at[0:1], one_hbm.at[0:1])
 
     loads[2].wait()
     out = dot(f2[...].reshape(256, 256), w2[...])
@@ -261,19 +265,21 @@
         for k, term in enumerate(edge_terms(lambda k: y2[c, :, k, :], 64)):
             xs2[k, c] = term
     x2 = send_x(1, xs2, xr2)
+    send_units(2)
     arrive(x2)
     x_split(y2, xr2, own2, (0, 1))
     z_terms(own2, zs2, range(4), 32)
-    z2 = [send_z(4, zs2, zr2, 0), send_z(5, zs2, zr2, pl.ds(1, 3))]
-    arrive(z2[0])
+    z2 = send_z(1, zs2, zr2, 0)
+    send_units(3)
+    arrive(z2)
     z_split(own2, zr2, 0, 32, f3, two.at[0])
-    store(two.at[0:1], two_hbm.at[0:1])
 
     loads[3].wait()
     y3[0] = dot(f3[...].reshape(64, 128), w3[...]).reshape(2, 32, 128)
     for k, term in enumerate(edge_terms(lambda k: y3[0, :, k, :], 32)):
         xs3[k, 0] = term
     x3 = send_x(2, xs3, xr3)
+    send_units(2)
     arrive(x3)
     x_split(y3, xr3, own3, (0,))
     for xb in range(2):
@@ -284,15 +290,16 @@
         zs3[2, xb] = even
         zs3[3, xb] = even + BE * (odd + AL * even)
     z3 = [
-        send(zs3.at[0:2], zr3.at[0:2], zsend.at[6, 0], zrecv.at[6, 0], {"gz": up}),
-        send(zs3.at[2:4], zr3.at[2:4], zsend.at[6, 1], zrecv.at[6, 1], {"gz": down}),
-        send(zs3.at[0:1], zr3b.at[0:1], zsend.at[7, 0], zrecv.at[7, 0], {"gz": up2}),
-        send(zs3.at[2:3], zr3b.at[1:2], zsend.at[7, 1], zrecv.at[7, 1], {"gz": down2}),
+        send(zs3.at[0:2], zr3.at[0:2], zsend.at[3, 0], zrecv.at[3, 0], {"gz": up}),
+        send(zs3.at[2:4], zr3.at[2:4], zsend.at[3, 1], zrecv.at[3, 1], {"gz": down}),
+        send(zs3.at[0:1], zr3b.at[0:1], zsend.at[4, 0], zrecv.at[4, 0], {"gz": up2}),
+        send(zs3.at[2:3], zr3b.at[1:2], zsend.at[4, 1], zrecv.at[4, 1], {"gz": down2}),
     ]
+    send_units(len(units))
+    z2 = send_z(2, zs2, zr2, pl.ds(1, 3))
     for g in (1, 2):
-        arrive(z1[g])
+        arrive(on_way[g])
         z_split(own1, zr1, g, 8, *bands(one, g))
-        store(one.at[2 * g - 1 : 2 * g + 1], one_hbm.at[2 * g - 1 : 2 * g + 1])
     arrive(z3)
     for xb in range(2):
         a, b, e, c = (zr3[k, xb] for k in range(4))
@@ -308,18 +315,22 @@
             else:
                 three[band - 1, 0] = low[:, lanes]
             three[band, 0] = high[:, lanes]
-    store(coarse, coarse_hbm)
-    store(three, three_hbm)
-    arrive(z2[1])
+    arrive(on_way[3])
+    z_split(own1, zr1, 3, 8, *bands(one, 3))
+    arrive(z2)
     for g in (1, 2, 3):
         z_split(own2, zr2, g, 32, *bands(two, g))
-    store(two.at[1:7], two_hbm.at[1:7])
-    arrive(z1[3])
-    z_split(own1, zr1, 3, 8, *bands(one, 3))
-    store(one.at[5:7], one_hbm.at[5:7])
     for copy in sent:
         copy.wait_send()
-    for copy in stores:
+
+
+def place(one, two, three, coarse, one_to, two_to, three_to, coarse_to, sem):
+    pairs = [(one.at[b], one_to.at[b]) for b in range(7)]
+    pairs += [(two, two_to), (three, three_to), (coarse, coarse_to)]
+    copies = [pltpu.make_async_copy(src, dst, sem.at[i]) for i, (src, dst) in enumerate(pairs)]
+    for copy in copies:
+        copy.start()
+    for copy in copies:
         copy.wait()
 
 
@@ -331,19 +342,28 @@
         (4, 8, 128, 128), (4, 4, 8, 128), (4, 4, 8, 128), (4, 8, 64, 256), (2, 4, 2, 64, 256), (2, 4, 2, 64, 256),
         (4, 64, 256), (2, 4, 64, 128), (4, 2, 4, 128), (4, 2, 4, 128), (4, 4, 32, 128), (2, 4, 2, 32, 128), (2, 4, 2, 32, 128),
         (2, 32, 128), (1, 2, 32, 128), (4, 1, 2, 128), (4, 1, 2, 128), (2, 2, 16, 128), (4, 2, 16, 128), (4, 2, 16, 128), (2, 2, 16, 128),
-    ] + shapes
+    ]
     dma = pltpu.SemaphoreType.DMA
     hbm = pl.BlockSpec(memory_space=pl.ANY)
-    return pl.pallas_call(
+    vmem = pl.BlockSpec(memory_space=pltpu.VMEM)
+    results = pl.pallas_call(
         functools.partial(kernel, nz, nx),
-        out_shape=tuple(jax.ShapeDtypeStruct(s, f32) for s in shapes),
+        out_shape=tuple(pltpu.VMEM(s, f32) for s in shapes),
         in_specs=[hbm] * 4,
-        out_specs=(hbm,) * 4,
+        out_specs=(vmem,) * 4,
         scratch_shapes=[pltpu.VMEM(s, f32) for s in scratch]
-        + [dma((4,)), dma((8,)), dma((3, 2)), dma((3, 2)), dma((8, 2)), dma((8, 2))],
+        + [dma((4,)), dma((3, 2)), dma((3, 2)), dma((5, 2)), dma((5, 2)), dma((12, 2)), dma((12, 2))],
         compiler_params=pltpu.CompilerParams(collective_id=0, has_side_effects=True),
         name="wavelet",
     )(velocity, *(jnp.asarray(band_matrix(n)) for n in (512, 256, 128)))
+    return pl.pallas_call(
+        place,
+        out_shape=tuple(jax.ShapeDtypeStruct(s, f32) for s in shapes),
+        in_specs=[vmem] * 4,
+        out_specs=(hbm,) * 4,
+        scratch_shapes=[dma((10,))],
+        name="place",
+    )(*(pltpu.with_memory_space_constraint(r, pltpu.VMEM) for r in results))
 
 
 def solution(mesh):

time: 58.5 us -> 48.4 us (0.83)
  Pallas kernels: 52.8 us -> 47.6 us
  local copies, waits for them, and re-layouts: 4.89 us -> 0 us
    pallas_call x1 -> x2, Pallas kernels: 52.8 us -> 47.6 us  [the longest x1 46.2 us: on_device(): pl.pallas_call(functools.partial(kernel, nz, nx), out_shape=tuple((pltpu....]
    unnamed x10 -> x0, local copies, waits for them, and re-layouts: 4.89 us -> none
where the time goes in v2:
time: 48.4 us; the launch traced here: 48.3 us
  Pallas kernels  47.6 us (98%)
  between operations  0.64 us (1%)
    pallas_call x1, Pallas kernels, on_device(): pl.pallas_call(functools.partial(kernel, nz, nx), out_shape=tuple((pltpu....  46.2 us
    pallas_call x1, Pallas kernels, on_device(): pl.pallas_call(place, out_shape=tuple((jax.ShapeDtypeStruct(s, f32) for s...  1.39 us

profile of v2, /device:TPU:1, one launch (start us, length us, event | category | flops | bytes accessed | tf_op | source)
XLA Modules:
  0.0 48.3 jit_solution(1188374483579210939)
XLA Ops:
  0.6 46.2 %wavelet.1 = (f32[7,4,64,256]{3,2,1,0:T(8,128)S(1)}, f32[7,2,32,128]{3,2,1,0:T(8,128)S(1)}, f32[7,1,16,64]{3,2,1,0:T(8,128)S(1)}, f32[1,16,64]{2,1,0:T(8,128)S(1)}) custom-call(f32[8,128,512]{2,1,0:T(8,128)} %v_hbm.1, f32[512,512]{1,0:T(8,128)} %constant.6.clone.w1_hbm, f32[256,256]{1,0:T(8,128)} %constant.7.clone.w2_hbm, f32[128,128]{1,0:T(8,128)} %constant.8.clone.w3_hbm), custom_call_target="tpu_custom_call" | custom-call | tf_op jit(solution)/shard_map/wavelet/pallas_call | solution.py:349
  46.9 1.4 %place.1 = (f32[7,4,64,256]{3,2,1,0:T(8,128)}, f32[7,2,32,128]{3,2,1,0:T(8,128)}, f32[7,1,16,64]{3,2,1,0:T(8,128)}, f32[1,16,64]{2,1,0:T(8,128)}) custom-call(f32[7,4,64,256]{3,2,1,0:T(8,128)S(1)} %get-tuple-element.8.one, f32[7,2,32,128]{3,2,1,0:T(8,128)S(1)} %get-tuple-element.9.two, f32[7,1,16,64]{3,2,1,0:T(8,128)S(1)} %get-tuple-element.10.three, ...), custom_call_target="tpu_custom_call" | custom-call | tf_op jit(solution)/shard_map/place/pallas_call | solution.py:359

commit v3 on v2

--- a/solution.py
+++ b/solution.py
@@ -102,15 +102,64 @@
     return s2, d2
 
 
+def deinterleave(n):
+    p = np.zeros((n, n), np.float32)
+    for j in range(n // 2):
+        p[2 * j, j] = p[2 * j + 1, n // 2 + j] = 1.0
+    return p
+
+
+def lift_lanes(x, pick):
+    even, odd = [], []
+    for b in range(x.shape[1] // 256):
+        block = x[:, 256 * b : 256 * b + 256]
+        parts = []
+        for _ in range(3):
+            parts.append(block.astype(jnp.bfloat16))
+            block = block - parts[-1].astype(jnp.float32)
+        out = sum(jnp.dot(part, pick, preferred_element_type=jnp.float32) for part in parts)
+        even.append(out[:, :128])
+        odd.append(out[:, 128:])
+    n = len(even)
+    lane = lax.broadcasted_iota(jnp.int32, even[0].shape, 1)
+
+    def following(v):
+        moved = [pltpu.roll(u, 127, 1) for u in v]
+        return moved if n == 1 else [jnp.where(lane == 127, moved[(i + 1) % n], moved[i]) for i in range(n)]
+
+    def preceding(v):
+        moved = [pltpu.roll(u, 1, 1) for u in v]
+        return moved if n == 1 else [jnp.where(lane == 0, moved[(i - 1) % n], moved[i]) for i in range(n)]
+
+    def step(v, factor, w, shifted):
+        return [p + factor * (q + r) for p, q, r in zip(v, w, shifted(w))]
+
+    d1 = step(odd, AL, even, following)
+    s1 = step(even, BE, d1, preceding)
+    d2 = step(d1, GA, s1, following)
+    s2 = step(s1, DE, d2, preceding)
+    return [KL * u for u in s2] + [KH * u for u in d2]
+
+
+def halo_effect(a, b, e, c):
+    first = (GA * BE) * a
+    before = a + GA * (b + BE * a)
+    q = AL * e
+    last = q + GA * (c + (2 * BE) * q)
+    last_but = (GA * BE) * q
+    low = (BE * a + DE * (before + first), DE * first, DE * last_but, BE * q + DE * (last_but + last))
+    return low, (first, last_but, last)
+
+
 def dot(x, w):
     return jnp.dot(x, w, precision=HIGHEST, preferred_element_type=jnp.float32)
 
 
 def kernel(
     nz, nx,
-    v_hbm, w1_hbm, w2_hbm, w3_hbm,
+    v_hbm, pick_hbm, w3_hbm,
     one, two, three, coarse,
-    f1, w1, w2, w3, y1, xs1, xr1, own1, zs1, zr1,
+    f1, pick, w3, y1, yz1, xs1, xr1, own1, zs1, zr1,
     f2, y2, xs2, xr2, own2, zs2, zr2,
     f3, y3, xs3, xr3, own3, zs3, zr3, zr3b,
     in_sem, xsend, xrecv, zsend, zrecv, usend, urecv,
@@ -129,7 +178,7 @@
     loads = [
         pltpu.make_async_copy(src, dst, in_sem.at[i])
         for i, (src, dst) in enumerate(
-            [(v_hbm, f1), (w1_hbm, w1), (w2_hbm, w2), (w3_hbm, w3)]
+            [(v_hbm, f1), (pick_hbm, pick), (w3_hbm, w3)]
         )
     ]
     for load in loads:
@@ -156,6 +205,12 @@
         return [
             send(zs.at[0, groups], zr.at[0, groups], zsend.at[slot, 0], zrecv.at[slot, 0], {"gz": up}),
             send(zs.at[1, groups], zr.at[1, groups], zsend.at[slot, 1], zrecv.at[slot, 1], {"gz": down}),
+        ]
+
+    def send_rows(slot, at):
+        return [
+            send(zs1.at[d, 0, :, at], zr1.at[d, 0, :, at], zsend.at[slot, d], zrecv.at[slot, d], {"gz": k})
+            for d, k in ((0, up), (1, down))
         ]
 
     units = [(g, k, r) for g in (1, 2, 3) for k in range(2) for r in range(2)]
@@ -176,25 +231,34 @@
         for copy in copies:
             copy.wait_recv()
 
-    def x_split(y, xr, own, columns):
-        planes, half = y.shape[1], y.shape[2] // 2
-        wide = max(1, y.shape[0] // 2)
+    def x_split(y, xr, put):
+        chunks, planes, half = y.shape[0], y.shape[1], y.shape[2] // 2
+        wide = max(1, chunks // 2)
 
         def plane(p):
-            for column in columns:
-                yb, at = column // wide, 128 * (column % wide)
-                even = y[column, p, pl.ds(0, half, stride=2), :]
-                odd = y[column, p, pl.ds(1, half, stride=2), :]
-                terms = [xr[k, column, pl.ds(p, 1), :] for k in range(4)]
+            for c in range(chunks):
+                even = y[c, p, pl.ds(0, half, stride=2), :]
+                odd = y[c, p, pl.ds(1, half, stride=2), :]
+                if xr is None:
+                    terms = [jnp.zeros((1, 128), jnp.float32)] * 4
+                else:
+                    terms = [xr[k, c, pl.ds(p, 1), :] for k in range(4)]
                 low, high = lift_rows(even, odd, *terms)
-                own[2 * yb, p, :, pl.ds(at, 128)] = low
-                own[2 * yb + 1, p, :, pl.ds(at, 128)] = high
+                lanes = pl.ds(128 * (c % wide), 128)
+                put(2 * (c // wide), p, lanes, low)
+                put(2 * (c // wide) + 1, p, lanes, high)
 
         if planes == 8:
             lax.fori_loop(0, planes, lambda p, _: (plane(p), 0)[1], 0)
         else:
             for p in range(planes):
                 plane(p)
+
+    def into(own):
+        def put(g, p, lanes, value):
+            own[g, p, :, lanes] = value
+
+        return put
 
     def z_terms(own, zs, groups, step):
         planes, rows = own.shape[1], own.shape[2]
@@ -226,62 +290,80 @@
     def bands(out, g):
         return out.at[2 * g - 1], out.at[2 * g]
 
+    loads[1].wait()
     loads[0].wait()
-    loads[1].wait()
     edges = edge_terms(lambda k: f1[:, k, :], f1.shape[1])
-    out = dot(jnp.concatenate(edges, 0), w1[...])
+    out = lift_lanes(jnp.concatenate(edges, 0), pick[...])
     for k in range(4):
         for c in range(4):
-            xs1[k, c] = out[8 * k : 8 * k + 8, 128 * c : 128 * c + 128]
+            xs1[k, c] = out[c][8 * k : 8 * k + 8]
+
+    def rows(i, _):
+        at = pl.ds(pl.multiple_of(32 * i, 32), 32)
+        terms = edge_terms(lambda k: f1[k, at, :], f1.shape[0])
+        out = lift_lanes(jnp.concatenate(terms, 0), pick[...])
+        for k in range(4):
+            for c in range(4):
+                yz1[c, k, at, :] = out[c][32 * k : 32 * k + 32]
+        return 0
+
+    lax.fori_loop(0, 4, rows, 0)
     pl.semaphore_wait(barrier, 6)
     x1 = send_x(0, xs1, xr1)
-    planes = f1.shape[0]
-    for yb in range(2):
-        lanes = pl.ds(256 * yb, 256)
-
-        def rows(i, _):
-            at = pl.ds(2 * i, 2)
-            out = dot(f1[at].reshape(256, 512), w1[:, lanes])
-            for c in range(2):
-                y1[2 * yb + c, at] = out[:, 128 * c : 128 * c + 128].reshape(2, 128, 128)
-            return 0
-
-        lax.fori_loop(0, planes // 2, rows, 0)
-        if yb == 0:
-            arrive(x1)
-        x_split(y1, xr1, own1, (2 * yb, 2 * yb + 1))
-        z_terms(own1, zs1, (2 * yb, 2 * yb + 1), 16)
-        if yb == 0:
-            z1 = send_z(0, zs1, zr1, 0)
-            send_units(3)
+
+    def put_terms(g, p, lanes, value):
+        zs1[p // 2, g, p % 2, :, lanes] = value
+
+    x_split(yz1, None, put_terms)
+    z1 = send_rows(0, pl.ds(8, 48))
+    arrive(x1)
+    for c in range(4):
+        g, lanes = 2 * (c // 2), pl.ds(128 * (c % 2), 128)
+        terms = [edge_terms(lambda i: xr1[k, c, i : i + 1, :], 8) for k in range(4)]
+        for p in range(4):
+            low, high = halo_effect(*(terms[k][p] for k in range(4)))
+            for r, effect in zip((0, 1, 62, 63), low):
+                zs1[p // 2, g, p % 2, r : r + 1, lanes] += effect
+            for r, effect in zip((0, 62, 63), high):
+                zs1[p // 2, g + 1, p % 2, r : r + 1, lanes] += effect
+    z1 += send_rows(1, pl.ds(0, 8)) + send_rows(2, pl.ds(56, 8))
+    send_units(4)
+
+    def plane(p, _):
+        out = lift_lanes(f1[p], pick[...])
+        for c in range(4):
+            y1[c, p] = out[c]
+        return 0
+
+    lax.fori_loop(0, f1.shape[0], plane, 0)
+    x_split(y1, xr1, into(own1))
 
     arrive(z1)
     z_split(own1, zr1, 0, 8, f2, one.at[0])
 
-    loads[2].wait()
-    out = dot(f2[...].reshape(256, 256), w2[...])
+    out = lift_lanes(f2[...].reshape(256, 256), pick[...])
     for c in range(2):
-        y2[c] = out[:, 128 * c : 128 * c + 128].reshape(4, 64, 128)
+        y2[c] = out[c].reshape(4, 64, 128)
         for k, term in enumerate(edge_terms(lambda k: y2[c, :, k, :], 64)):
             xs2[k, c] = term
     x2 = send_x(1, xs2, xr2)
-    send_units(2)
+    send_units(3)
     arrive(x2)
-    x_split(y2, xr2, own2, (0, 1))
+    x_split(y2, xr2, into(own2))
     z_terms(own2, zs2, range(4), 32)
-    z2 = send_z(1, zs2, zr2, 0)
+    z2 = send_z(3, zs2, zr2, 0)
     send_units(3)
     arrive(z2)
     z_split(own2, zr2, 0, 32, f3, two.at[0])
 
-    loads[3].wait()
+    loads[2].wait()
     y3[0] = dot(f3[...].reshape(64, 128), w3[...]).reshape(2, 32, 128)
     for k, term in enumerate(edge_terms(lambda k: y3[0, :, k, :], 32)):
         xs3[k, 0] = term
     x3 = send_x(2, xs3, xr3)
     send_units(2)
     arrive(x3)
-    x_split(y3, xr3, own3, (0,))
+    x_split(y3, xr3, into(own3))
     for xb in range(2):
         even, odd = own3[xb, 0], own3[xb, 1]
         a = odd + AL * even
@@ -290,13 +372,13 @@
         zs3[2, xb] = even
         zs3[3, xb] = even + BE * (odd + AL * even)
     z3 = [
-        send(zs3.at[0:2], zr3.at[0:2], zsend.at[3, 0], zrecv.at[3, 0], {"gz": up}),
-        send(zs3.at[2:4], zr3.at[2:4], zsend.at[3, 1], zrecv.at[3, 1], {"gz": down}),
-        send(zs3.at[0:1], zr3b.at[0:1], zsend.at[4, 0], zrecv.at[4, 0], {"gz": up2}),
-        send(zs3.at[2:3], zr3b.at[1:2], zsend.at[4, 1], zrecv.at[4, 1], {"gz": down2}),
+        send(zs3.at[0:2], zr3.at[0:2], zsend.at[5, 0], zrecv.at[5, 0], {"gz": up}),
+        send(zs3.at[2:4], zr3.at[2:4], zsend.at[5, 1], zrecv.at[5, 1], {"gz": down}),
+        send(zs3.at[0:1], zr3b.at[0:1], zsend.at[6, 0], zrecv.at[6, 0], {"gz": up2}),
+        send(zs3.at[2:3], zr3b.at[1:2], zsend.at[6, 1], zrecv.at[6, 1], {"gz": down2}),
     ]
     send_units(len(units))
-    z2 = send_z(2, zs2, zr2, pl.ds(1, 3))
+    z2 = send_z(4, zs2, zr2, pl.ds(1, 3))
     for g in (1, 2):
         arrive(on_way[g])
         z_split(own1, zr1, g, 8, *bands(one, g))
@@ -338,8 +420,8 @@
     f32 = jnp.float32
     shapes = [(7, 4, 64, 256), (7, 2, 32, 128), (7, 1, 16, 64), (1, 16, 64)]
     scratch = [
-        (8, 128, 512), (512, 512), (256, 256), (128, 128),
-        (4, 8, 128, 128), (4, 4, 8, 128), (4, 4, 8, 128), (4, 8, 64, 256), (2, 4, 2, 64, 256), (2, 4, 2, 64, 256),
+        (8, 128, 512), None, (128, 128),
+        (4, 8, 128, 128), (4, 4, 128, 128), (4, 4, 8, 128), (4, 4, 8, 128), (4, 8, 64, 256), (2, 4, 2, 64, 256), (2, 4, 2, 64, 256),
         (4, 64, 256), (2, 4, 64, 128), (4, 2, 4, 128), (4, 2, 4, 128), (4, 4, 32, 128), (2, 4, 2, 32, 128), (2, 4, 2, 32, 128),
         (2, 32, 128), (1, 2, 32, 128), (4, 1, 2, 128), (4, 1, 2, 128), (2, 2, 16, 128), (4, 2, 16, 128), (4, 2, 16, 128), (2, 2, 16, 128),
     ]
@@ -349,13 +431,13 @@
     results = pl.pallas_call(
         functools.partial(kernel, nz, nx),
         out_shape=tuple(pltpu.VMEM(s, f32) for s in shapes),
-        in_specs=[hbm] * 4,
+        in_specs=[hbm] * 3,
         out_specs=(vmem,) * 4,
-        scratch_shapes=[pltpu.VMEM(s, f32) for s in scratch]
-        + [dma((4,)), dma((3, 2)), dma((3, 2)), dma((5, 2)), dma((5, 2)), dma((12, 2)), dma((12, 2))],
+        scratch_shapes=[pltpu.VMEM(s, f32) if s else pltpu.VMEM((256, 256), jnp.bfloat16) for s in scratch]
+        + [dma((3,)), dma((3, 2)), dma((3, 2)), dma((7, 2)), dma((7, 2)), dma((12, 2)), dma((12, 2))],
         compiler_params=pltpu.CompilerParams(collective_id=0, has_side_effects=True),
         name="wavelet",
-    )(velocity, *(jnp.asarray(band_matrix(n)) for n in (512, 256, 128)))
+    )(velocity, jnp.asarray(deinterleave(256), jnp.bfloat16), jnp.asarray(band_matrix(128)))
     return pl.pallas_call(
         place,
         out_shape=tuple(jax.ShapeDtypeStruct(s, f32) for s in shapes),

time: 48.4 us -> 46.3 us (0.957)
  Pallas kernels: 47.6 us -> 45.5 us
    pallas_call x1, Pallas kernels: 46.2 us -> 44.1 us  [on_device(): pl.pallas_call(functools.partial(kernel, nz, nx), out_shape=tuple((pltpu....]
where the time goes in v3:
time: 46.3 us; the launch traced here: 46.2 us
  Pallas kernels  45.5 us (98%)
  between operations  0.64 us (1%)
    pallas_call x1, Pallas kernels, on_device(): pl.pallas_call(functools.partial(kernel, nz, nx), out_shape=tuple((pltpu....  44.1 us
    pallas_call x1, Pallas kernels, on_device(): pl.pallas_call(place, out_shape=tuple((jax.ShapeDtypeStruct(s, f32) for s...  1.39 us

profile of v3, /device:TPU:1, one launch (start us, length us, event | category | flops | bytes accessed | tf_op | source)
XLA Modules:
  0.0 46.2 jit_solution(14031229456728273607)
XLA Ops:
  0.6 44.1 %wavelet.1 = (f32[7,4,64,256]{3,2,1,0:T(8,128)S(1)}, f32[7,2,32,128]{3,2,1,0:T(8,128)S(1)}, f32[7,1,16,64]{3,2,1,0:T(8,128)S(1)}, f32[1,16,64]{2,1,0:T(8,128)S(1)}) custom-call(f32[8,128,512]{2,1,0:T(8,128)} %v_hbm.1, bf16[256,256]{1,0:T(8,128)(2,1)} %constant.4.clone.pick_hbm, f32[128,128]{1,0:T(8,128)} %constant.5.clone.w3_hbm), custom_call_target="tpu_custom_call" | custom-call | tf_op jit(solution)/shard_map/wavelet/pallas_call | solution.py:431
  44.8 1.4 %place.1 = (f32[7,4,64,256]{3,2,1,0:T(8,128)}, f32[7,2,32,128]{3,2,1,0:T(8,128)}, f32[7,1,16,64]{3,2,1,0:T(8,128)}, f32[1,16,64]{2,1,0:T(8,128)}) custom-call(f32[7,4,64,256]{3,2,1,0:T(8,128)S(1)} %get-tuple-element.8.one, f32[7,2,32,128]{3,2,1,0:T(8,128)S(1)} %get-tuple-element.9.two, f32[7,1,16,64]{3,2,1,0:T(8,128)S(1)} %get-tuple-element.10.three, ...), custom_call_target="tpu_custom_call" | custom-call | tf_op jit(solution)/shard_map/place/pallas_call | solution.py:441

commit v4 on v3

--- a/solution.py
+++ b/solution.py
@@ -159,7 +159,7 @@
     nz, nx,
     v_hbm, pick_hbm, w3_hbm,
     one, two, three, coarse,
-    f1, pick, w3, y1, yz1, xs1, xr1, own1, zs1, zr1,
+    f1, pick, w3, y1, yz1, xz1, xs1, xr1, own1, zs1, zr1,
     f2, y2, xs2, xr2, own2, zs2, zr2,
     f3, y3, xs3, xr3, own3, zs3, zr3, zr3b,
     in_sem, xsend, xrecv, zsend, zrecv, usend, urecv,
@@ -169,17 +169,22 @@
     up, down = lax.rem(iz + 1, nz), lax.rem(iz + nz - 1, nz)
     up2, down2 = lax.rem(iz + 2, nz), lax.rem(iz + nz - 2, nz)
 
+    near = lax.rem(iz, 2)
+    sides = [(d, {"gz": lax.rem(iz + nz + 1 - 2 * d, nz)}) for d in (1 - near, near)]
+
     barrier = pltpu.get_barrier_semaphore()
     for k in (right, left):
         pl.semaphore_signal(barrier, inc=1, device_id={"gx": k}, device_id_type=MESH)
     for k in (up, down, up2, down2):
         pl.semaphore_signal(barrier, inc=1, device_id={"gz": k}, device_id_type=MESH)
 
+    parts = (0, 3, 1, 2)
     loads = [
-        pltpu.make_async_copy(src, dst, in_sem.at[i])
-        for i, (src, dst) in enumerate(
-            [(v_hbm, f1), (pick_hbm, pick), (w3_hbm, w3)]
-        )
+        pltpu.make_async_copy(v_hbm.at[:, pl.ds(32 * k, 32)], f1.at[:, pl.ds(32 * k, 32)], in_sem.at[i])
+        for i, k in enumerate(parts)
+    ]
+    loads += [
+        pltpu.make_async_copy(src, dst, in_sem.at[i]) for i, src, dst in ((4, pick_hbm, pick), (5, w3_hbm, w3))
     ]
     for load in loads:
         load.start()
@@ -201,31 +206,27 @@
             send(xs.at[2:4], xr.at[2:4], xsend.at[level, 1], xrecv.at[level, 1], {"gx": left}),
         ]
 
-    def send_z(slot, zs, zr, groups):
+    def send_z(slot, zs, zr, *at, which=(0, 1)):
         return [
-            send(zs.at[0, groups], zr.at[0, groups], zsend.at[slot, 0], zrecv.at[slot, 0], {"gz": up}),
-            send(zs.at[1, groups], zr.at[1, groups], zsend.at[slot, 1], zrecv.at[slot, 1], {"gz": down}),
-        ]
-
-    def send_rows(slot, at):
-        return [
-            send(zs1.at[d, 0, :, at], zr1.at[d, 0, :, at], zsend.at[slot, d], zrecv.at[slot, d], {"gz": k})
-            for d, k in ((0, up), (1, down))
+            send(zs.at[(d,) + at], zr.at[(d,) + at], zsend.at[slot, d], zrecv.at[slot, d], device)
+            for d, device in (sides[w] for w in which)
         ]
 
     units = [(g, k, r) for g in (1, 2, 3) for k in range(2) for r in range(2)]
     pending = list(units)
     on_way = {1: [], 2: [], 3: []}
 
-    def send_units(count):
-        for _ in range(min(count, len(pending))):
-            g, k, r = pending.pop(0)
+    def send_units(count, which=(0, 1)):
+        done = len(units) - len(pending)
+        for i in range(done, done + count):
+            g, k, r = units[i]
             at = pl.ds(32 * r, 32)
-            for d, device in ((0, {"gz": up}), (1, {"gz": down})):
-                i = units.index((g, k, r))
+            for d, device in (sides[w] for w in which):
                 on_way[g].append(
                     send(zs1.at[d, g, k, at], zr1.at[d, g, k, at], usend.at[i, d], urecv.at[i, d], device)
                 )
+        if which[-1] == 1:
+            del pending[:count]
 
     def arrive(copies):
         for copy in copies:
@@ -233,7 +234,6 @@
 
     def x_split(y, xr, put):
         chunks, planes, half = y.shape[0], y.shape[1], y.shape[2] // 2
-        wide = max(1, chunks // 2)
 
         def plane(p):
             for c in range(chunks):
@@ -244,19 +244,18 @@
                 else:
                     terms = [xr[k, c, pl.ds(p, 1), :] for k in range(4)]
                 low, high = lift_rows(even, odd, *terms)
-                lanes = pl.ds(128 * (c % wide), 128)
-                put(2 * (c // wide), p, lanes, low)
-                put(2 * (c // wide) + 1, p, lanes, high)
+                put(c, 0, p, low)
+                put(c, 1, p, high)
 
         if planes == 8:
-            lax.fori_loop(0, planes, lambda p, _: (plane(p), 0)[1], 0)
+            lax.fori_loop(0, planes // 2, lambda i, _: (plane(2 * i), plane(2 * i + 1), 0)[2], 0)
         else:
             for p in range(planes):
                 plane(p)
 
-    def into(own):
-        def put(g, p, lanes, value):
-            own[g, p, :, lanes] = value
+    def into(own, wide):
+        def put(c, xb, p, value):
+            own[2 * (c // wide) + xb, p, :, pl.ds(128 * (c % wide), 128)] = value
 
         return put
 
@@ -290,32 +289,45 @@
     def bands(out, g):
         return out.at[2 * g - 1], out.at[2 * g]
 
-    loads[1].wait()
-    loads[0].wait()
+    for i, part in enumerate(parts):
+        loads[i].wait()
+        at = pl.ds(32 * part, 32)
+        for c in range(4):
+            terms = edge_terms(lambda k: f1[k, at, pl.ds(128 * c, 128)], f1.shape[0])
+            for k in range(4):
+                yz1[c, k, at, :] = terms[k]
+
+    def put_raw(c, xb, p, value):
+        xz1[xb, p, :, pl.ds(128 * c, 128)] = value
+
+    x_split(yz1, None, put_raw)
     edges = edge_terms(lambda k: f1[:, k, :], f1.shape[1])
-    out = lift_lanes(jnp.concatenate(edges, 0), pick[...])
+    loads[4].wait()
+
+    def put_terms(xb, out):
+        for c in range(4):
+            for p in range(4):
+                zs1[p // 2, 2 * (c // 2) + xb, p % 2, :, pl.ds(128 * (c % 2), 128)] = out[c][64 * p : 64 * p + 64]
+
+    out = lift_lanes(jnp.concatenate([xz1[0].reshape(256, 512), *edges], 0), pick[...])
     for k in range(4):
         for c in range(4):
-            xs1[k, c] = out[c][8 * k : 8 * k + 8]
-
-    def rows(i, _):
-        at = pl.ds(pl.multiple_of(32 * i, 32), 32)
-        terms = edge_terms(lambda k: f1[k, at, :], f1.shape[0])
-        out = lift_lanes(jnp.concatenate(terms, 0), pick[...])
-        for k in range(4):
-            for c in range(4):
-                yz1[c, k, at, :] = out[c][32 * k : 32 * k + 32]
-        return 0
-
-    lax.fori_loop(0, 4, rows, 0)
+            xs1[k, c] = out[c][256 + 8 * k : 264 + 8 * k]
+    put_terms(0, out)
     pl.semaphore_wait(barrier, 6)
     x1 = send_x(0, xs1, xr1)
-
-    def put_terms(g, p, lanes, value):
-        zs1[p // 2, g, p % 2, :, lanes] = value
-
-    x_split(yz1, None, put_terms)
-    z1 = send_rows(0, pl.ds(8, 48))
+    z1 = send_z(0, zs1, zr1, 0, slice(None), pl.ds(8, 48))
+    put_terms(1, lift_lanes(xz1[1].reshape(256, 512), pick[...]))
+
+    def rows(i, _):
+        at = pl.ds(2 * i, 2)
+        out = lift_lanes(f1[at].reshape(256, 512), pick[...])
+        for c in range(4):
+            y1[c, at] = out[c].reshape(2, 128, 128)
+        return 0
+
+    lax.fori_loop(0, f1.shape[0] // 2, rows, 0)
+
     arrive(x1)
     for c in range(4):
         g, lanes = 2 * (c // 2), pl.ds(128 * (c % 2), 128)
@@ -326,17 +338,9 @@
                 zs1[p // 2, g, p % 2, r : r + 1, lanes] += effect
             for r, effect in zip((0, 62, 63), high):
                 zs1[p // 2, g + 1, p % 2, r : r + 1, lanes] += effect
-    z1 += send_rows(1, pl.ds(0, 8)) + send_rows(2, pl.ds(56, 8))
-    send_units(4)
-
-    def plane(p, _):
-        out = lift_lanes(f1[p], pick[...])
-        for c in range(4):
-            y1[c, p] = out[c]
-        return 0
-
-    lax.fori_loop(0, f1.shape[0], plane, 0)
-    x_split(y1, xr1, into(own1))
+    z1 += send_z(1, zs1, zr1, 0, slice(None), pl.ds(0, 8)) + send_z(2, zs1, zr1, 0, slice(None), pl.ds(56, 8))
+    send_units(3)
+    x_split(y1, xr1, into(own1, 2))
 
     arrive(z1)
     z_split(own1, zr1, 0, 8, f2, one.at[0])
@@ -349,21 +353,21 @@
     x2 = send_x(1, xs2, xr2)
     send_units(3)
     arrive(x2)
-    x_split(y2, xr2, into(own2))
+    x_split(y2, xr2, into(own2, 1))
     z_terms(own2, zs2, range(4), 32)
     z2 = send_z(3, zs2, zr2, 0)
     send_units(3)
     arrive(z2)
     z_split(own2, zr2, 0, 32, f3, two.at[0])
 
-    loads[2].wait()
+    loads[5].wait()
     y3[0] = dot(f3[...].reshape(64, 128), w3[...]).reshape(2, 32, 128)
     for k, term in enumerate(edge_terms(lambda k: y3[0, :, k, :], 32)):
         xs3[k, 0] = term
     x3 = send_x(2, xs3, xr3)
     send_units(2)
     arrive(x3)
-    x_split(y3, xr3, into(own3))
+    x_split(y3, xr3, into(own3, 1))
     for xb in range(2):
         even, odd = own3[xb, 0], own3[xb, 1]
         a = odd + AL * even
@@ -377,8 +381,10 @@
         send(zs3.at[0:1], zr3b.at[0:1], zsend.at[6, 0], zrecv.at[6, 0], {"gz": up2}),
         send(zs3.at[2:3], zr3b.at[1:2], zsend.at[6, 1], zrecv.at[6, 1], {"gz": down2}),
     ]
-    send_units(len(units))
-    z2 = send_z(4, zs2, zr2, pl.ds(1, 3))
+    z2 = []
+    for w in range(2):
+        send_units(1, (w,))
+        z2 += send_z(4, zs2, zr2, pl.ds(1, 3), which=(w,))
     for g in (1, 2):
         arrive(on_way[g])
         z_split(own1, zr1, g, 8, *bands(one, g))
@@ -421,7 +427,7 @@
     shapes = [(7, 4, 64, 256), (7, 2, 32, 128), (7, 1, 16, 64), (1, 16, 64)]
     scratch = [
         (8, 128, 512), None, (128, 128),
-        (4, 8, 128, 128), (4, 4, 128, 128), (4, 4, 8, 128), (4, 4, 8, 128), (4, 8, 64, 256), (2, 4, 2, 64, 256), (2, 4, 2, 64, 256),
+        (4, 8, 128, 128), (4, 4, 128, 128), (2, 4, 64, 512), (4, 4, 8, 128), (4, 4, 8, 128), (4, 8, 64, 256), (2, 4, 2, 64, 256), (2, 4, 2, 64, 256),
         (4, 64, 256), (2, 4, 64, 128), (4, 2, 4, 128), (4, 2, 4, 128), (4, 4, 32, 128), (2, 4, 2, 32, 128), (2, 4, 2, 32, 128),
         (2, 32, 128), (1, 2, 32, 128), (4, 1, 2, 128), (4, 1, 2, 128), (2, 2, 16, 128), (4, 2, 16, 128), (4, 2, 16, 128), (2, 2, 16, 128),
     ]
@@ -434,7 +440,7 @@
         in_specs=[hbm] * 3,
         out_specs=(vmem,) * 4,
         scratch_shapes=[pltpu.VMEM(s, f32) if s else pltpu.VMEM((256, 256), jnp.bfloat16) for s in scratch]
-        + [dma((3,)), dma((3, 2)), dma((3, 2)), dma((7, 2)), dma((7, 2)), dma((12, 2)), dma((12, 2))],
+        + [dma((6,)), dma((3, 2)), dma((3, 2)), dma((7, 2)), dma((7, 2)), dma((12, 2)), dma((12, 2))],
         compiler_params=pltpu.CompilerParams(collective_id=0, has_side_effects=True),
         name="wavelet",
     )(velocity, jnp.asarray(deinterleave(256), jnp.bfloat16), jnp.asarray(band_matrix(128)))

time: 46.3 us -> 44.2 us (0.955)
  Pallas kernels: 45.5 us -> 43.4 us
    pallas_call x1, Pallas kernels: 44.1 us -> 42 us  [on_device(): pl.pallas_call(functools.partial(kernel, nz, nx), out_shape=tuple((pltpu....]
where the time goes in v4:
time: 44.2 us; the launch traced here: 44.1 us
  Pallas kernels  43.4 us (98%)
  between operations  0.64 us (1%)
    pallas_call x1, Pallas kernels, on_device(): pl.pallas_call(functools.partial(kernel, nz, nx), out_shape=tuple((pltpu....  42 us
    pallas_call x1, Pallas kernels, on_device(): pl.pallas_call(place, out_shape=tuple((jax.ShapeDtypeStruct(s, f32) for s...  1.39 us

profile of v4, /device:TPU:1, one launch (start us, length us, event | category | flops | bytes accessed | tf_op | source)
XLA Modules:
  0.0 44.1 jit_solution(17332219270410877810)
XLA Ops:
  0.6 42.0 %wavelet.1 = (f32[7,4,64,256]{3,2,1,0:T(8,128)S(1)}, f32[7,2,32,128]{3,2,1,0:T(8,128)S(1)}, f32[7,1,16,64]{3,2,1,0:T(8,128)S(1)}, f32[1,16,64]{2,1,0:T(8,128)S(1)}) custom-call(f32[8,128,512]{2,1,0:T(8,128)} %v_hbm.1, bf16[256,256]{1,0:T(8,128)(2,1)} %constant.4.clone.pick_hbm, f32[128,128]{1,0:T(8,128)} %constant.5.clone.w3_hbm), custom_call_target="tpu_custom_call" | custom-call | tf_op jit(solution)/shard_map/wavelet/pallas_call | solution.py:437
  42.7 1.4 %place.1 = (f32[7,4,64,256]{3,2,1,0:T(8,128)}, f32[7,2,32,128]{3,2,1,0:T(8,128)}, f32[7,1,16,64]{3,2,1,0:T(8,128)}, f32[1,16,64]{2,1,0:T(8,128)}) custom-call(f32[7,4,64,256]{3,2,1,0:T(8,128)S(1)} %get-tuple-element.8.one, f32[7,2,32,128]{3,2,1,0:T(8,128)S(1)} %get-tuple-element.9.two, f32[7,1,16,64]{3,2,1,0:T(8,128)S(1)} %get-tuple-element.10.three, ...), custom_call_target="tpu_custom_call" | custom-call | tf_op jit(solution)/shard_map/place/pallas_call | solution.py:447

commit v5 on v4

--- a/solution.py
+++ b/solution.py
@@ -37,6 +37,8 @@
 KH = 1.230174104914001
 SCALE = (KL, KH)
 
+UNITS = (4, 3, 3, 2)
+
 MESH = pl.DeviceIdType.MESH
 HIGHEST = lax.Precision.HIGHEST
 
@@ -160,9 +162,9 @@
     v_hbm, pick_hbm, w3_hbm,
     one, two, three, coarse,
     f1, pick, w3, y1, yz1, xz1, xs1, xr1, own1, zs1, zr1,
-    f2, y2, xs2, xr2, own2, zs2, zr2,
-    f3, y3, xs3, xr3, own3, zs3, zr3, zr3b,
-    in_sem, xsend, xrecv, zsend, zrecv, usend, urecv,
+    f2, y2, yz2, xs2, xr2, cs2, cr2, own2, zs2, zr2,
+    f3, y3, yz3, xs3, xr3, cs3, cr3, cr3b, own3, zs3, zr3, zr3b,
+    in_sem, xsend, xrecv, csend, crecv, zsend, zrecv, usend, urecv,
 ):
     iz, ix = lax.axis_index("gz"), lax.axis_index("gx")
     right, left = lax.rem(ix + 1, nx), lax.rem(ix + nx - 1, nx)
@@ -173,10 +175,11 @@
     sides = [(d, {"gz": lax.rem(iz + nz + 1 - 2 * d, nz)}) for d in (1 - near, near)]
 
     barrier = pltpu.get_barrier_semaphore()
-    for k in (right, left):
-        pl.semaphore_signal(barrier, inc=1, device_id={"gx": k}, device_id_type=MESH)
+    others = [{"gx": k} for k in (right, left)]
     for k in (up, down, up2, down2):
-        pl.semaphore_signal(barrier, inc=1, device_id={"gz": k}, device_id_type=MESH)
+        others += [{"gz": k}, {"gz": k, "gx": right}, {"gz": k, "gx": left}]
+    for k in others:
+        pl.semaphore_signal(barrier, inc=1, device_id=k, device_id_type=MESH)
 
     parts = (0, 3, 1, 2)
     loads = [
@@ -210,6 +213,13 @@
         return [
             send(zs.at[(d,) + at], zr.at[(d,) + at], zsend.at[slot, d], zrecv.at[slot, d], device)
             for d, device in (sides[w] for w in which)
+        ]
+
+    def send_corners(slot, cs, cr, above, below):
+        return [
+            send(cs.at[d, h], cr.at[d, h], csend.at[slot, d, h], crecv.at[slot, d, h], {"gz": k, "gx": m})
+            for d, k in ((0, above), (1, below))
+            for h, m in ((0, right), (1, left))
         ]
 
     units = [(g, k, r) for g in (1, 2, 3) for k in range(2) for r in range(2)]
@@ -259,18 +269,6 @@
 
         return put
 
-    def z_terms(own, zs, groups, step):
-        planes, rows = own.shape[1], own.shape[2]
-        for g in groups:
-            def chunk(i, _):
-                at = pl.ds(pl.multiple_of(i * step, step), step)
-                terms = edge_terms(lambda k: own[g, k, at, :], planes)
-                for k in range(4):
-                    zs[k // 2, g, k % 2, at, :] = terms[k]
-                return 0
-
-            lax.fori_loop(0, rows // step, chunk, 0)
-
     def z_split(own, zr, g, step, low_to, high_to):
         planes, rows = own.shape[1], own.shape[2]
 
@@ -314,7 +312,7 @@
         for c in range(4):
             xs1[k, c] = out[c][256 + 8 * k : 264 + 8 * k]
     put_terms(0, out)
-    pl.semaphore_wait(barrier, 6)
+    pl.semaphore_wait(barrier, len(others))
     x1 = send_x(0, xs1, xr1)
     z1 = send_z(0, zs1, zr1, 0, slice(None), pl.ds(8, 48))
     put_terms(1, lift_lanes(xz1[1].reshape(256, 512), pick[...]))
@@ -339,58 +337,99 @@
             for r, effect in zip((0, 62, 63), high):
                 zs1[p // 2, g + 1, p % 2, r : r + 1, lanes] += effect
     z1 += send_z(1, zs1, zr1, 0, slice(None), pl.ds(0, 8)) + send_z(2, zs1, zr1, 0, slice(None), pl.ds(56, 8))
-    send_units(3)
+    send_units(UNITS[0])
     x_split(y1, xr1, into(own1, 2))
 
     arrive(z1)
     z_split(own1, zr1, 0, 8, f2, one.at[0])
+
+    def add_halo(to, terms, wanted):
+        low, high = halo_effect(*terms)
+        n = to(0).shape[0]
+        if 0 in wanted:
+            for r, effect in zip((0, 1, n - 2, n - 1), low):
+                to(0)[r : r + 1, :] += effect
+        if 1 in wanted:
+            for r, effect in zip((0, n - 2, n - 1), high):
+                to(1)[r : r + 1, :] += effect
 
     out = lift_lanes(f2[...].reshape(256, 256), pick[...])
     for c in range(2):
         y2[c] = out[c].reshape(4, 64, 128)
         for k, term in enumerate(edge_terms(lambda k: y2[c, :, k, :], 64)):
             xs2[k, c] = term
-    x2 = send_x(1, xs2, xr2)
-    send_units(3)
+        for k, term in enumerate(edge_terms(lambda k: y2[c, k], 4)):
+            yz2[c, k] = term
+        for t in range(4):
+            for k, term in enumerate(edge_terms(lambda i: xs2[t, c, i : i + 1, :], 4)):
+                cs2[k // 2, t // 2, k % 2, t % 2, c : c + 1, :] = term
+
+    def put_terms2(c, xb, p, value):
+        zs2[p // 2, 2 * c + xb, p % 2] = value
+
+    x2 = send_x(1, xs2, xr2) + send_corners(0, cs2, cr2, up, down)
+    x_split(yz2, None, put_terms2)
+    z2 = send_z(3, zs2, zr2, 0)
+    send_units(UNITS[1])
+
+    def add_halo2(c, wanted):
+        for d in range(2):
+            for k in range(2):
+                add_halo(
+                    lambda xb: zr2.at[d, 2 * c + xb, k],
+                    [cr2[d, t // 2, k, t % 2, c : c + 1, :] for t in range(4)],
+                    wanted,
+                )
+
     arrive(x2)
     x_split(y2, xr2, into(own2, 1))
-    z_terms(own2, zs2, range(4), 32)
-    z2 = send_z(3, zs2, zr2, 0)
-    send_units(3)
     arrive(z2)
+    add_halo2(0, (0,))
     z_split(own2, zr2, 0, 32, f3, two.at[0])
+
+    def terms3(even, odd):
+        a = odd + AL * even
+        return a, even + BE * (AL * even + a), even, even + BE * a
 
     loads[5].wait()
     y3[0] = dot(f3[...].reshape(64, 128), w3[...]).reshape(2, 32, 128)
     for k, term in enumerate(edge_terms(lambda k: y3[0, :, k, :], 32)):
         xs3[k, 0] = term
-    x3 = send_x(2, xs3, xr3)
-    send_units(2)
+    for k, term in enumerate(terms3(y3[0, 0], y3[0, 1])):
+        yz3[0, k] = term
+    for t in range(4):
+        for k, term in enumerate(terms3(xs3[t, 0, 0:1, :], xs3[t, 0, 1:2, :])):
+            cs3[k // 2, t // 2, k % 2, t % 2 : t % 2 + 1, :] = term
+
+    def put_terms3(c, xb, p, value):
+        zs3[p // 2, p % 2, xb] = value
+
+    x3 = send_x(2, xs3, xr3) + send_corners(1, cs3, cr3, up, down)
+    x3 += [
+        send(cs3.at[d, h, 0], cr3b.at[d, h], csend.at[2, d, h], crecv.at[2, d, h], {"gz": k, "gx": m})
+        for d, k in ((0, up2), (1, down2))
+        for h, m in ((0, right), (1, left))
+    ]
+    x_split(yz3, None, put_terms3)
+    z3 = send_z(5, zs3, zr3)
+    z3 += [
+        send(zs3.at[d, 0], zr3b.at[d], zsend.at[6, d], zrecv.at[6, d], {"gz": k})
+        for d, k in ((0, up2), (1, down2))
+    ]
+    send_units(UNITS[2])
+    z2 = send_z(4, zs2, zr2, pl.ds(1, 3))
+    for w in range(2):
+        send_units(UNITS[3], (w,))
+
     arrive(x3)
     x_split(y3, xr3, into(own3, 1))
+    arrive(z3)
+    for d in range(2):
+        for k in range(2):
+            add_halo(lambda xb: zr3.at[d, k, xb], [cr3[d, t // 2, k, t % 2 : t % 2 + 1, :] for t in range(4)], (0, 1))
+        add_halo(lambda xb: zr3b.at[d, xb], [cr3b[d, t // 2, t % 2 : t % 2 + 1, :] for t in range(4)], (0, 1))
     for xb in range(2):
-        even, odd = own3[xb, 0], own3[xb, 1]
-        a = odd + AL * even
-        zs3[0, xb] = a
-        zs3[1, xb] = even + BE * (AL * even + a)
-        zs3[2, xb] = even
-        zs3[3, xb] = even + BE * (odd + AL * even)
-    z3 = [
-        send(zs3.at[0:2], zr3.at[0:2], zsend.at[5, 0], zrecv.at[5, 0], {"gz": up}),
-        send(zs3.at[2:4], zr3.at[2:4], zsend.at[5, 1], zrecv.at[5, 1], {"gz": down}),
-        send(zs3.at[0:1], zr3b.at[0:1], zsend.at[6, 0], zrecv.at[6, 0], {"gz": up2}),
-        send(zs3.at[2:3], zr3b.at[1:2], zsend.at[6, 1], zrecv.at[6, 1], {"gz": down2}),
-    ]
-    z2 = []
-    for w in range(2):
-        send_units(1, (w,))
-        z2 += send_z(4, zs2, zr2, pl.ds(1, 3), which=(w,))
-    for g in (1, 2):
-        arrive(on_way[g])
-        z_split(own1, zr1, g, 8, *bands(one, g))
-    arrive(z3)
-    for xb in range(2):
-        a, b, e, c = (zr3[k, xb] for k in range(4))
+        a, b, e, c = (zr3[k // 2, k % 2, xb] for k in range(4))
         b = b + BE * zr3b[0, xb]
         c = c + (AL * BE) * zr3b[1, xb]
         low, high = lift_planes([own3[xb, 0], own3[xb, 1]], a, b, e, c)
@@ -403,11 +442,17 @@
             else:
                 three[band - 1, 0] = low[:, lanes]
             three[band, 0] = high[:, lanes]
+
+    for g in (1, 2):
+        arrive(on_way[g])
+        z_split(own1, zr1, g, 8, *bands(one, g))
+    arrive(z2)
+    add_halo2(0, (1,))
+    add_halo2(1, (0, 1))
+    for g in (1, 2, 3):
+        z_split(own2, zr2, g, 32, *bands(two, g))
     arrive(on_way[3])
     z_split(own1, zr1, 3, 8, *bands(one, 3))
-    arrive(z2)
-    for g in (1, 2, 3):
-        z_split(own2, zr2, g, 32, *bands(two, g))
     for copy in sent:
         copy.wait_send()
 
@@ -428,8 +473,11 @@
     scratch = [
         (8, 128, 512), None, (128, 128),
         (4, 8, 128, 128), (4, 4, 128, 128), (2, 4, 64, 512), (4, 4, 8, 128), (4, 4, 8, 128), (4, 8, 64, 256), (2, 4, 2, 64, 256), (2, 4, 2, 64, 256),
-        (4, 64, 256), (2, 4, 64, 128), (4, 2, 4, 128), (4, 2, 4, 128), (4, 4, 32, 128), (2, 4, 2, 32, 128), (2, 4, 2, 32, 128),
-        (2, 32, 128), (1, 2, 32, 128), (4, 1, 2, 128), (4, 1, 2, 128), (2, 2, 16, 128), (4, 2, 16, 128), (4, 2, 16, 128), (2, 2, 16, 128),
+        (4, 64, 256), (2, 4, 64, 128), (2, 4, 64, 128), (4, 2, 4, 128), (4, 2, 4, 128),
+        (2, 2, 2, 2, 2, 128), (2, 2, 2, 2, 2, 128), (4, 4, 32, 128), (2, 4, 2, 32, 128), (2, 4, 2, 32, 128),
+        (2, 32, 128), (1, 2, 32, 128), (1, 4, 32, 128), (4, 1, 2, 128), (4, 1, 2, 128),
+        (2, 2, 2, 2, 128), (2, 2, 2, 2, 128), (2, 2, 2, 128), (2, 2, 16, 128),
+        (2, 2, 2, 16, 128), (2, 2, 2, 16, 128), (2, 2, 16, 128),
     ]
     dma = pltpu.SemaphoreType.DMA
     hbm = pl.BlockSpec(memory_space=pl.ANY)
@@ -440,7 +488,7 @@
         in_specs=[hbm] * 3,
         out_specs=(vmem,) * 4,
         scratch_shapes=[pltpu.VMEM(s, f32) if s else pltpu.VMEM((256, 256), jnp.bfloat16) for s in scratch]
-        + [dma((6,)), dma((3, 2)), dma((3, 2)), dma((7, 2)), dma((7, 2)), dma((12, 2)), dma((12, 2))],
+        + [dma((6,)), dma((3, 2)), dma((3, 2)), dma((3, 2, 2)), dma((3, 2, 2)), dma((7, 2)), dma((7, 2)), dma((12, 2)), dma((12, 2))],
         compiler_params=pltpu.CompilerParams(collective_id=0, has_side_effects=True),
         name="wavelet",
     )(velocity, jnp.asarray(deinterleave(256), jnp.bfloat16), jnp.asarray(band_matrix(128)))

time: 44.2 us -> 47.4 us (1.072)
  Pallas kernels: 43.4 us -> 46.6 us
    pallas_call x1, Pallas kernels: 42 us -> 45.2 us  [on_device(): pl.pallas_call(functools.partial(kernel, nz, nx), out_shape=tuple((pltpu....]
where the time goes in v5:
time: 47.4 us; the launch traced here: 47.2 us
  Pallas kernels  46.6 us (98%)
  between operations  0.64 us (1%)
    pallas_call x1, Pallas kernels, on_device(): pl.pallas_call(functools.partial(kernel, nz, nx), out_shape=tuple((pltpu....  45.2 us
    pallas_call x1, Pallas kernels, on_device(): pl.pallas_call(place, out_shape=tuple((jax.ShapeDtypeStruct(s, f32) for s...  1.39 us

profile of v5, /device:TPU:1, one launch (start us, length us, event | category | flops | bytes accessed | tf_op | source)
XLA Modules:
  0.0 47.2 jit_solution(65308490773086717)
XLA Ops:
  0.6 45.2 %wavelet.1 = (f32[7,4,64,256]{3,2,1,0:T(8,128)S(1)}, f32[7,2,32,128]{3,2,1,0:T(8,128)S(1)}, f32[7,1,16,64]{3,2,1,0:T(8,128)S(1)}, f32[1,16,64]{2,1,0:T(8,128)S(1)}) custom-call(f32[8,128,512]{2,1,0:T(8,128)} %v_hbm.1, bf16[256,256]{1,0:T(8,128)(2,1)} %constant.4.clone.pick_hbm, f32[128,128]{1,0:T(8,128)} %constant.5.clone.w3_hbm), custom_call_target="tpu_custom_call" | custom-call | tf_op jit(solution)/shard_map/wavelet/pallas_call | solution.py:485
  45.8 1.4 %place.1 = (f32[7,4,64,256]{3,2,1,0:T(8,128)}, f32[7,2,32,128]{3,2,1,0:T(8,128)}, f32[7,1,16,64]{3,2,1,0:T(8,128)}, f32[1,16,64]{2,1,0:T(8,128)}) custom-call(f32[7,4,64,256]{3,2,1,0:T(8,128)S(1)} %get-tuple-element.8.one, f32[7,2,32,128]{3,2,1,0:T(8,128)S(1)} %get-tuple-element.9.two, f32[7,1,16,64]{3,2,1,0:T(8,128)S(1)} %get-tuple-element.10.three, ...), custom_call_target="tpu_custom_call" | custom-call | tf_op jit(solution)/shard_map/place/pallas_call | solution.py:495

commit v6 on v4

--- a/solution.py
+++ b/solution.py
@@ -37,6 +37,10 @@
 KH = 1.230174104914001
 SCALE = (KL, KH)
 
+UNITS = (2, 3, 2, 3, 2)
+
+OWN_FIRST = 2
+
 MESH = pl.DeviceIdType.MESH
 HIGHEST = lax.Precision.HIGHEST
 
@@ -157,9 +161,9 @@
 
 def kernel(
     nz, nx,
-    v_hbm, pick_hbm, w3_hbm,
+    v_hbm, pick_hbm, w2_hbm, w3_hbm,
     one, two, three, coarse,
-    f1, pick, w3, y1, yz1, xz1, xs1, xr1, own1, zs1, zr1,
+    f1, pick, w2, w3, y1, yz1, xz1, xs1, xr1, own1, zs1, zr1,
     f2, y2, xs2, xr2, own2, zs2, zr2,
     f3, y3, xs3, xr3, own3, zs3, zr3, zr3b,
     in_sem, xsend, xrecv, zsend, zrecv, usend, urecv,
@@ -175,7 +179,7 @@
     barrier = pltpu.get_barrier_semaphore()
     for k in (right, left):
         pl.semaphore_signal(barrier, inc=1, device_id={"gx": k}, device_id_type=MESH)
-    for k in (up, down, up2, down2):
+    for k in (up, down):
         pl.semaphore_signal(barrier, inc=1, device_id={"gz": k}, device_id_type=MESH)
 
     parts = (0, 3, 1, 2)
@@ -184,7 +188,7 @@
         for i, k in enumerate(parts)
     ]
     loads += [
-        pltpu.make_async_copy(src, dst, in_sem.at[i]) for i, src, dst in ((4, pick_hbm, pick), (5, w3_hbm, w3))
+        pltpu.make_async_copy(src, dst, in_sem.at[i]) for i, src, dst in ((4, pick_hbm, pick), (5, w3_hbm, w3), (6, w2_hbm, w2))
     ]
     for load in loads:
         load.start()
@@ -232,7 +236,7 @@
         for copy in copies:
             copy.wait_recv()
 
-    def x_split(y, xr, put):
+    def x_split(y, xr, put, some=None):
         chunks, planes, half = y.shape[0], y.shape[1], y.shape[2] // 2
 
         def plane(p):
@@ -250,7 +254,7 @@
         if planes == 8:
             lax.fori_loop(0, planes // 2, lambda i, _: (plane(2 * i), plane(2 * i + 1), 0)[2], 0)
         else:
-            for p in range(planes):
+            for p in range(planes) if some is None else some:
                 plane(p)
 
     def into(own, wide):
@@ -300,24 +304,30 @@
     def put_raw(c, xb, p, value):
         xz1[xb, p, :, pl.ds(128 * c, 128)] = value
 
-    x_split(yz1, None, put_raw)
+    def terms_of(xb, planes, extra=()):
+        rows = [xz1[xb, p] for p in planes]
+        out = lift_lanes(jnp.concatenate([*rows, *extra], 0), pick[...])
+        for c in range(4):
+            for i, p in enumerate(planes):
+                zs1[p // 2, 2 * (c // 2) + xb, lax.rem(p, 2), :, pl.ds(128 * (c % 2), 128)] = out[c][64 * i : 64 * i + 64]
+        return [out_c[64 * len(planes) :] for out_c in out]
+
+    pairs = [[2 * d, 2 * d + 1] for d, _ in sides]
+    x_split(yz1, None, put_raw, pairs[0])
     edges = edge_terms(lambda k: f1[:, k, :], f1.shape[1])
     loads[4].wait()
-
-    def put_terms(xb, out):
-        for c in range(4):
-            for p in range(4):
-                zs1[p // 2, 2 * (c // 2) + xb, p % 2, :, pl.ds(128 * (c % 2), 128)] = out[c][64 * p : 64 * p + 64]
-
-    out = lift_lanes(jnp.concatenate([xz1[0].reshape(256, 512), *edges], 0), pick[...])
+    out = terms_of(0, pairs[0], edges)
     for k in range(4):
         for c in range(4):
-            xs1[k, c] = out[c][256 + 8 * k : 264 + 8 * k]
-    put_terms(0, out)
-    pl.semaphore_wait(barrier, 6)
+            xs1[k, c] = out[c][8 * k : 8 * k + 8]
+    pl.semaphore_wait(barrier, 4)
     x1 = send_x(0, xs1, xr1)
-    z1 = send_z(0, zs1, zr1, 0, slice(None), pl.ds(8, 48))
-    put_terms(1, lift_lanes(xz1[1].reshape(256, 512), pick[...]))
+    inner = (0, slice(None), pl.ds(8, 48))
+    z1 = send_z(0, zs1, zr1, *inner, which=(0,))
+    x_split(yz1, None, put_raw, pairs[1])
+    terms_of(0, pairs[1])
+    z1 += send_z(0, zs1, zr1, *inner, which=(1,))
+    terms_of(1, range(4))
 
     def rows(i, _):
         at = pl.ds(2 * i, 2)
@@ -326,8 +336,7 @@
             y1[c, at] = out[c].reshape(2, 128, 128)
         return 0
 
-    lax.fori_loop(0, f1.shape[0] // 2, rows, 0)
-
+    lax.fori_loop(0, OWN_FIRST, rows, 0)
     arrive(x1)
     for c in range(4):
         g, lanes = 2 * (c // 2), pl.ds(128 * (c % 2), 128)
@@ -339,24 +348,29 @@
             for r, effect in zip((0, 62, 63), high):
                 zs1[p // 2, g + 1, p % 2, r : r + 1, lanes] += effect
     z1 += send_z(1, zs1, zr1, 0, slice(None), pl.ds(0, 8)) + send_z(2, zs1, zr1, 0, slice(None), pl.ds(56, 8))
-    send_units(3)
+    send_units(UNITS[0])
+    lax.fori_loop(OWN_FIRST, f1.shape[0] // 2, rows, 0)
     x_split(y1, xr1, into(own1, 2))
 
     arrive(z1)
     z_split(own1, zr1, 0, 8, f2, one.at[0])
 
-    out = lift_lanes(f2[...].reshape(256, 256), pick[...])
+    loads[6].wait()
+    edges = edge_terms(lambda k: f2[:, k, :], f2.shape[1])
+    out = dot(jnp.concatenate(edges, 0), w2[...])
+    for k in range(4):
+        for c in range(2):
+            xs2[k, c] = out[4 * k : 4 * k + 4, 128 * c : 128 * c + 128]
+    x2 = send_x(1, xs2, xr2)
+    send_units(UNITS[1])
+    out = dot(f2[...].reshape(256, 256), w2[...])
     for c in range(2):
-        y2[c] = out[c].reshape(4, 64, 128)
-        for k, term in enumerate(edge_terms(lambda k: y2[c, :, k, :], 64)):
-            xs2[k, c] = term
-    x2 = send_x(1, xs2, xr2)
-    send_units(3)
+        y2[c] = out[:, 128 * c : 128 * c + 128].reshape(4, 64, 128)
     arrive(x2)
     x_split(y2, xr2, into(own2, 1))
     z_terms(own2, zs2, range(4), 32)
     z2 = send_z(3, zs2, zr2, 0)
-    send_units(3)
+    send_units(UNITS[2])
     arrive(z2)
     z_split(own2, zr2, 0, 32, f3, two.at[0])
 
@@ -365,32 +379,30 @@
     for k, term in enumerate(edge_terms(lambda k: y3[0, :, k, :], 32)):
         xs3[k, 0] = term
     x3 = send_x(2, xs3, xr3)
-    send_units(2)
+    send_units(UNITS[3])
     arrive(x3)
     x_split(y3, xr3, into(own3, 1))
     for xb in range(2):
         even, odd = own3[xb, 0], own3[xb, 1]
         a = odd + AL * even
-        zs3[0, xb] = a
-        zs3[1, xb] = even + BE * (AL * even + a)
-        zs3[2, xb] = even
-        zs3[3, xb] = even + BE * (odd + AL * even)
-    z3 = [
-        send(zs3.at[0:2], zr3.at[0:2], zsend.at[5, 0], zrecv.at[5, 0], {"gz": up}),
-        send(zs3.at[2:4], zr3.at[2:4], zsend.at[5, 1], zrecv.at[5, 1], {"gz": down}),
-        send(zs3.at[0:1], zr3b.at[0:1], zsend.at[6, 0], zrecv.at[6, 0], {"gz": up2}),
-        send(zs3.at[2:3], zr3b.at[1:2], zsend.at[6, 1], zrecv.at[6, 1], {"gz": down2}),
+        zs3[0, 0, xb] = a
+        zs3[0, 1, xb] = even + BE * (AL * even + a)
+        zs3[1, 0, xb] = even
+        zs3[1, 1, xb] = even + BE * a
+    z3 = send_z(5, zs3, zr3) + [
+        send(zs3.at[d, 0], zr3b.at[d], zsend.at[6, d], zrecv.at[6, d], {"gz": k})
+        for d, k in ((0, up2), (1, down2))
     ]
     z2 = []
     for w in range(2):
-        send_units(1, (w,))
+        send_units(UNITS[4], (w,))
         z2 += send_z(4, zs2, zr2, pl.ds(1, 3), which=(w,))
     for g in (1, 2):
         arrive(on_way[g])
         z_split(own1, zr1, g, 8, *bands(one, g))
     arrive(z3)
     for xb in range(2):
-        a, b, e, c = (zr3[k, xb] for k in range(4))
+        a, b, e, c = (zr3[k // 2, k % 2, xb] for k in range(4))
         b = b + BE * zr3b[0, xb]
         c = c + (AL * BE) * zr3b[1, xb]
         low, high = lift_planes([own3[xb, 0], own3[xb, 1]], a, b, e, c)
@@ -426,10 +438,10 @@
     f32 = jnp.float32
     shapes = [(7, 4, 64, 256), (7, 2, 32, 128), (7, 1, 16, 64), (1, 16, 64)]
     scratch = [
-        (8, 128, 512), None, (128, 128),
+        (8, 128, 512), None, (256, 256), (128, 128),
         (4, 8, 128, 128), (4, 4, 128, 128), (2, 4, 64, 512), (4, 4, 8, 128), (4, 4, 8, 128), (4, 8, 64, 256), (2, 4, 2, 64, 256), (2, 4, 2, 64, 256),
         (4, 64, 256), (2, 4, 64, 128), (4, 2, 4, 128), (4, 2, 4, 128), (4, 4, 32, 128), (2, 4, 2, 32, 128), (2, 4, 2, 32, 128),
-        (2, 32, 128), (1, 2, 32, 128), (4, 1, 2, 128), (4, 1, 2, 128), (2, 2, 16, 128), (4, 2, 16, 128), (4, 2, 16, 128), (2, 2, 16, 128),
+        (2, 32, 128), (1, 2, 32, 128), (4, 1, 2, 128), (4, 1, 2, 128), (2, 2, 16, 128), (2, 2, 2, 16, 128), (2, 2, 2, 16, 128), (2, 2, 16, 128),
     ]
     dma = pltpu.SemaphoreType.DMA
     hbm = pl.BlockSpec(memory_space=pl.ANY)
@@ -437,13 +449,13 @@
     results = pl.pallas_call(
         functools.partial(kernel, nz, nx),
         out_shape=tuple(pltpu.VMEM(s, f32) for s in shapes),
-        in_specs=[hbm] * 3,
+        in_specs=[hbm] * 4,
         out_specs=(vmem,) * 4,
         scratch_shapes=[pltpu.VMEM(s, f32) if s else pltpu.VMEM((256, 256), jnp.bfloat16) for s in scratch]
-        + [dma((6,)), dma((3, 2)), dma((3, 2)), dma((7, 2)), dma((7, 2)), dma((12, 2)), dma((12, 2))],
+        + [dma((7,)), dma((3, 2)), dma((3, 2)), dma((7, 2)), dma((7, 2)), dma((12, 2)), dma((12, 2))],
         compiler_params=pltpu.CompilerParams(collective_id=0, has_side_effects=True),
         name="wavelet",
-    )(velocity, jnp.asarray(deinterleave(256), jnp.bfloat16), jnp.asarray(band_matrix(128)))
+    )(velocity, jnp.asarray(deinterleave(256), jnp.bfloat16), jnp.asarray(band_matrix(256)), jnp.asarray(band_matrix(128)))
     return pl.pallas_call(
         place,
         out_shape=tuple(jax.ShapeDtypeStruct(s, f32) for s in shapes),

time: 44.2 us -> 43.3 us (0.980)
  Pallas kernels: 43.4 us -> 42.5 us
    pallas_call x1, Pallas kernels: 42 us -> 41.1 us  [on_device(): pl.pallas_call(functools.partial(kernel, nz, nx), out_shape=tuple((pltpu....]
where the time goes in v6:
time: 43.3 us; the launch traced here: 43.1 us
  Pallas kernels  42.5 us (98%)
  between operations  0.64 us (1%)
    pallas_call x1, Pallas kernels, on_device(): pl.pallas_call(functools.partial(kernel, nz, nx), out_shape=tuple((pltpu....  41.1 us
    pallas_call x1, Pallas kernels, on_device(): pl.pallas_call(place, out_shape=tuple((jax.ShapeDtypeStruct(s, f32) for s...  1.39 us

profile of v6, /device:TPU:1, one launch (start us, length us, event | category | flops | bytes accessed | tf_op | source)
XLA Modules:
  0.0 43.1 jit_solution(4292409830705115843)
XLA Ops:
  0.6 41.1 %wavelet.1 = (f32[7,4,64,256]{3,2,1,0:T(8,128)S(1)}, f32[7,2,32,128]{3,2,1,0:T(8,128)S(1)}, f32[7,1,16,64]{3,2,1,0:T(8,128)S(1)}, f32[1,16,64]{2,1,0:T(8,128)S(1)}) custom-call(f32[8,128,512]{2,1,0:T(8,128)} %v_hbm.1, bf16[256,256]{1,0:T(8,128)(2,1)} %constant.6.clone.pick_hbm, f32[256,256]{1,0:T(8,128)} %constant.7.clone.w2_hbm, ...), custom_call_target="tpu_custom_call" | custom-call | tf_op jit(solution)/shard_map/wavelet/pallas_call | solution.py:449
  41.7 1.4 %place.1 = (f32[7,4,64,256]{3,2,1,0:T(8,128)}, f32[7,2,32,128]{3,2,1,0:T(8,128)}, f32[7,1,16,64]{3,2,1,0:T(8,128)}, f32[1,16,64]{2,1,0:T(8,128)}) custom-call(f32[7,4,64,256]{3,2,1,0:T(8,128)S(1)} %get-tuple-element.8.one, f32[7,2,32,128]{3,2,1,0:T(8,128)S(1)} %get-tuple-element.9.two, f32[7,1,16,64]{3,2,1,0:T(8,128)S(1)} %get-tuple-element.10.three, ...), custom_call_target="tpu_custom_call" | custom-call | tf_op jit(solution)/shard_map/place/pallas_call | solution.py:459

commit v7 on v6

--- a/solution.py
+++ b/solution.py
@@ -37,7 +37,7 @@
 KH = 1.230174104914001
 SCALE = (KL, KH)
 
-UNITS = (2, 3, 2, 3, 2)
+UNITS = (2, 3, 2, 4, 1)
 
 OWN_FIRST = 2
 
@@ -348,7 +348,8 @@
             for r, effect in zip((0, 62, 63), high):
                 zs1[p // 2, g + 1, p % 2, r : r + 1, lanes] += effect
     z1 += send_z(1, zs1, zr1, 0, slice(None), pl.ds(0, 8)) + send_z(2, zs1, zr1, 0, slice(None), pl.ds(56, 8))
-    send_units(UNITS[0])
+    for w in range(2):
+        send_units(UNITS[0], (w,))
     lax.fori_loop(OWN_FIRST, f1.shape[0] // 2, rows, 0)
     x_split(y1, xr1, into(own1, 2))
 
@@ -362,7 +363,8 @@
         for c in range(2):
             xs2[k, c] = out[4 * k : 4 * k + 4, 128 * c : 128 * c + 128]
     x2 = send_x(1, xs2, xr2)
-    send_units(UNITS[1])
+    for w in range(2):
+        send_units(UNITS[1], (w,))
     out = dot(f2[...].reshape(256, 256), w2[...])
     for c in range(2):
         y2[c] = out[:, 128 * c : 128 * c + 128].reshape(4, 64, 128)
@@ -370,7 +372,8 @@
     x_split(y2, xr2, into(own2, 1))
     z_terms(own2, zs2, range(4), 32)
     z2 = send_z(3, zs2, zr2, 0)
-    send_units(UNITS[2])
+    for w in range(2):
+        send_units(UNITS[2], (w,))
     arrive(z2)
     z_split(own2, zr2, 0, 32, f3, two.at[0])
 
@@ -379,7 +382,8 @@
     for k, term in enumerate(edge_terms(lambda k: y3[0, :, k, :], 32)):
         xs3[k, 0] = term
     x3 = send_x(2, xs3, xr3)
-    send_units(UNITS[3])
+    for w in range(2):
+        send_units(UNITS[3], (w,))
     arrive(x3)
     x_split(y3, xr3, into(own3, 1))
     for xb in range(2):

time: 43.3 us -> 43.3 us (level)
  no operation moved by 1% of the time
where the time goes in v7:
time: 43.3 us; the launch traced here: 43.1 us
  Pallas kernels  42.5 us (98%)
  between operations  0.64 us (1%)
    pallas_call x1, Pallas kernels, on_device(): pl.pallas_call(functools.partial(kernel, nz, nx), out_shape=tuple((pltpu....  41.1 us
    pallas_call x1, Pallas kernels, on_device(): pl.pallas_call(place, out_shape=tuple((jax.ShapeDtypeStruct(s, f32) for s...  1.39 us

profile of v7, /device:TPU:1, one launch (start us, length us, event | category | flops | bytes accessed | tf_op | source)
XLA Modules:
  0.0 43.1 jit_solution(1897723029886269667)
XLA Ops:
  0.6 41.1 %wavelet.1 = (f32[7,4,64,256]{3,2,1,0:T(8,128)S(1)}, f32[7,2,32,128]{3,2,1,0:T(8,128)S(1)}, f32[7,1,16,64]{3,2,1,0:T(8,128)S(1)}, f32[1,16,64]{2,1,0:T(8,128)S(1)}) custom-call(f32[8,128,512]{2,1,0:T(8,128)} %v_hbm.1, bf16[256,256]{1,0:T(8,128)(2,1)} %constant.6.clone.pick_hbm, f32[256,256]{1,0:T(8,128)} %constant.7.clone.w2_hbm, ...), custom_call_target="tpu_custom_call" | custom-call | tf_op jit(solution)/shard_map/wavelet/pallas_call | solution.py:453
  41.7 1.4 %place.1 = (f32[7,4,64,256]{3,2,1,0:T(8,128)}, f32[7,2,32,128]{3,2,1,0:T(8,128)}, f32[7,1,16,64]{3,2,1,0:T(8,128)}, f32[1,16,64]{2,1,0:T(8,128)}) custom-call(f32[7,4,64,256]{3,2,1,0:T(8,128)S(1)} %get-tuple-element.8.one, f32[7,2,32,128]{3,2,1,0:T(8,128)S(1)} %get-tuple-element.9.two, f32[7,1,16,64]{3,2,1,0:T(8,128)S(1)} %get-tuple-element.10.three, ...), custom_call_target="tpu_custom_call" | custom-call | tf_op jit(solution)/shard_map/place/pallas_call | solution.py:463
